TPU v7x, 128 devices: a whole 4x4x4 slice. The times are simulated.
128 devices in a mesh: row: 8 (over y, core), col: 16 (over x, z).
Axes of the slice: x: 4, y: 4, z: 4, core: 2. Of those that a mesh axis runs over, the one named last changes fastest.
Arguments:
- tensor_tiles: bfloat16 [512, 128, 128, 128], P(('row', 'col')), may hold values from -384 to 384
- tile_mode1: int32 [512], P(('row', 'col')), may hold values from 0 to 1023, as said below
- tile_mode2: int32 [512], P(('row', 'col')), may hold values from 0 to 127
- tile_mode3: int32 [512], P(('row', 'col')), may hold values from 0 to 63
- factor_mode2: bfloat16 [48, 16384], P(None, 'col'), may hold values from -1 to 1
- factor_mode3: bfloat16 [48, 8192], P(None, 'row'), may hold values from -1 to 1
Outputs:
- factor_mode1: float32 [48, 131072], P(None, ('row', 'col'))
Inputs may be any that keep to these rules, and one draw needn't show every extreme that they name: `tile_mode1`: tiles at positions g*64 to (g+1)*64 - 1 have mode-1 blocks in g*128 to (g+1)*128 - 1; the 4 tiles at positions d*4 to (d+1)*4 - 1 have mode-1 blocks in distinct groups of 8 consecutive blocks (block // 8 all different).
All inputs are finite; a program needn't handle non-finite values.
Results may differ from a plain program's by a relative error of at most 0.0003.
Values may be sent and summed in bfloat16 or wider, within the bound.
No kernel may reach another device: no remote copies, remote signals or barrier semaphores. Data moves between devices by JAX's collectives and lax.ppermute only.
A program may use at most 128 MiB of HBM per device.

v0:
```python
import jax
import jax.numpy as jnp
from jax import lax
from jax.sharding import PartitionSpec as P

IB_DEV = 8


ridge_term = 0.5


def body(tensor_tiles, tile_mode1, tile_mode2, tile_mode3, factor_mode2, factor_mode3):
    rank_count = factor_mode2.shape[0]
    tile_edge = tensor_tiles.shape[1]
    gram_two = lax.psum(
        jnp.dot(factor_mode2, factor_mode2.T, preferred_element_type=jnp.float32), "col"
    )
    gram_three = lax.psum(
        jnp.dot(factor_mode3, factor_mode3.T, preferred_element_type=jnp.float32), "row"
    )
    system = gram_two * gram_three + ridge_term * jnp.eye(rank_count, dtype=jnp.float32)
    full_two = lax.all_gather(factor_mode2, "col", axis=1, tiled=True)
    full_three = lax.all_gather(factor_mode3, "row", axis=1, tiled=True)
    mode2_rows = jnp.transpose(
        full_two.reshape(rank_count, -1, tile_edge)[:, tile_mode2], (1, 0, 2)
    )
    mode3_rows = jnp.transpose(
        full_three.reshape(rank_count, -1, tile_edge)[:, tile_mode3], (1, 0, 2)
    )
    contracted = jnp.einsum(
        "trc,tabc->trab", mode3_rows, tensor_tiles, preferred_element_type=jnp.float32
    )
    tile_rows = jnp.einsum(
        "trab,trb->tra", contracted, mode2_rows.astype(jnp.float32), precision=lax.Precision.HIGHEST
    )
    col_count = lax.axis_size("col")
    row_blocks = IB_DEV * col_count
    local_blocks = tile_mode1 - lax.axis_index("row") * row_blocks
    selector = (local_blocks[:, None] == jnp.arange(row_blocks, dtype=jnp.int32)[None, :]).astype(
        jnp.float32
    )
    row_partials = jnp.einsum("tra,tb->rba", tile_rows, selector, precision=lax.Precision.HIGHEST)
    row_partials = row_partials.reshape(rank_count, row_blocks * tile_edge)
    right_side = lax.psum_scatter(row_partials, "col", scatter_dimension=1, tiled=True)
    cholesky_factor = jnp.linalg.cholesky(system)
    middle = lax.linalg.triangular_solve(cholesky_factor, right_side, left_side=True, lower=True)
    return lax.linalg.triangular_solve(
        cholesky_factor, middle, left_side=True, lower=True, transpose_a=True
    )


def solution(mesh):
    in_specs = (
        P(("row", "col"), None, None, None),
        P(("row", "col")),
        P(("row", "col")),
        P(("row", "col")),
        P(None, "col"),
        P(None, "row"),
    )
    out_specs = P(None, ("row", "col"))
    return jax.shard_map(body, mesh=mesh, in_specs=in_specs, out_specs=out_specs, check_vma=False)
```

profile of v0, /device:TPU:0, one launch (start us, length us, event | category | flops | bytes accessed | tf_op | source)
XLA Modules:
  0.0 194.9 jit_solution(6708601685298031785)
XLA Ops:
  6.5 0.0 all-gather.2.cloned.1.call-start
  6.5 0.7 all-gather.2.cloned.1.call-update
  7.3 0.0 reduce-scatter.2.cloned.1.call-start
  7.3 0.7 compare_select_fusion.1
  8.0 14.2 %all_gather.6 = bf16[48,8192]{1,0:T(8,128)(2,1)S(1)} all-gather(bf16[48,1024]{1,0:T(8,128)(2,1)} %param.11), channel_id=1, replica_groups=mesh['row'=8,'col'=16] {'row'}, dimensions={1}, use_global_device_ids=true | all-gather | bytes 884736 | tf_op jit(solution)/shard_map/all_gather | solution.py:23
  22.2 0.1 copy_bitcast_fusion.2
  22.3 0.6 gather_fusion
  22.9 0.7 compare_select_fusion
  23.6 0.7 broadcast_subtract_fusion
  24.2 12.1 %fusion.6 = f32[4,48,128,128]{3,1,2,0:T(8,128)} fusion(bf16[4,128,128,128]{3,2,1,0:T(8,128)(2,1)} %param.6, bf16[4,48,128]{2,1,0:T(8,128)(2,1)S(1)} %gather_fusion), kind=kOutput, calls=%fused_computation.11 | convolution fusion | flops 805306368 | bytes 29409280 | tf_op jit(solution)/shard_map/trc,tabc->trab/dot_general | solution.py:30
  36.3 19.6 %all-gather.2.cloned.1.call-done = bf16[48,16384]{1,0:T(8,128)(2,1)} async-done(((bf16[48,1024]{1,0:T(8,128)(2,1)}), bf16[48,16384]{1,0:T(8,128)(2,1)}) %all-gather.2.cloned.1.call-update) | async-done | bytes 1572880 | tf_op jit(solution)/shard_map/all_gather | solution.py:22
  55.9 1.7 copy_bitcast_fusion.1
  57.6 0.6 gather_fusion.1
  58.1 0.0 copy-start.1
  58.1 0.0 copy-start
  58.2 16.7 %fusion = f32[4,48,1,128]{3,2,1,0:T(1,128)S(1)} fusion(f32[4,48,128,128]{3,1,2,0:T(8,128)} %fusion.6, bf16[4,48,128,1]{2,1,0,3:T(8,128)(2,1)S(1)} %bitcast.47), kind=kOutput, calls=%fused_computation.2 | convolution fusion | flops 37748736 | bytes 12730368 | tf_op jit(solution)/shard_map/trab,trb->tra/dot_general | solution.py:33
  74.9 1.5 fusion.2
  76.4 3.5 %copy.30 = f32[6,8,128,128]{3,1,2,0:T(8,128)} copy(f32[6,8,128,128]{3,2,1,0:T(8,128)S(1)} %bitcast.46) | data formatting | bytes 6291456
  79.8 0.0 reduce-scatter.2.cloned.1.call-update
  79.9 0.0 copy-done.1
  79.9 0.1 fusion.17
  80.0 72.5 %psum.14 = f32[48,48]{1,0:T(8,128)S(1)} all-reduce(f32[48,48]{1,0:T(8,128)S(1)} %fusion.17), channel_id=1, replica_groups=mesh['row'=8,'col'=16] {'col'}, use_global_device_ids=true, to_apply=%region_0.0 | all-reduce | flops 2304 | bytes 18432 | tf_op jit(solution)/shard_map/psum | solution.py:15
  152.5 0.0 copy-done
  152.5 0.1 fusion.18
  152.7 23.6 %psum.15 = f32[48,48]{1,0:T(8,128)S(1)} all-reduce(f32[48,48]{1,0:T(8,128)S(1)} %fusion.18), channel_id=1, replica_groups=mesh['row'=8,'col'=16] {'row'}, use_global_device_ids=true, to_apply=%region_1.0 | all-reduce | flops 2304 | bytes 18432 | tf_op jit(solution)/shard_map/psum | solution.py:18
  176.3 0.1 copy.9
  176.4 4.4 %cholesky.16 = f32[48,48]{1,0:T(8,128)S(1)} custom-call(f32[48,48]{1,0:T(8,128)S(1)} %fusion.13), custom_call_target="Cholesky" | custom-call | tf_op jit(solution)/shard_map/jit(cholesky)/cholesky | solution.py:45
  180.8 0.6 compare_reduce_fusion
  181.4 0.7 fusion.8
  182.1 3.7 %custom-call.8 = f32[1,48,48]{1,2,0:T(8,128)S(1)} custom-call(f32[1,48,48]{2,1,0:T(8,128)S(1)} %fusion.8), custom_call_target="InvertDiagBlocksLowerTriangular" | custom-call | tf_op jit(solution)/shard_map/triangular_solve | solution.py:47
  185.8 1.3 fusion.11
  187.1 1.0 fusion.9
  (6 shorter events, 0.1 us)
Async XLA Ops:
  6.5 49.4 %all-gather.2.cloned.1.call-start = ((), (), s32[]{:S(2)}) async-start(), calls=%async_computation.1 | async-start | bytes 1671168 | tf_op jit(solution)/shard_map/all_gather | solution.py:22
  7.3 178.5 %reduce-scatter.2.cloned.1.call-start = ((), (), s32[]{:S(2)}) async-start(), calls=%async_computation.2 | async-start | bytes 3342336 | tf_op jit(solution)/shard_map/reduce_scatter | solution.py:44
  58.1 21.7 %copy-start.1 = (bf16[48,1024]{1,0:T(8,128)(2,1)S(1)}, bf16[48,1024]{1,0:T(8,128)(2,1)}, u32[]{:S(2)}) copy-start(bf16[48,1024]{1,0:T(8,128)(2,1)} %param.10) | copy-start | bytes 294916
  58.1 94.4 %copy-start = (bf16[48,1024]{1,0:T(8,128)(2,1)S(1)}, bf16[48,1024]{1,0:T(8,128)(2,1)}, u32[]{:S(2)}) copy-start(bf16[48,1024]{1,0:T(8,128)(2,1)} %param.11) | copy-start | bytes 294916
Sparse Core Ops, SparseCore 0:
  9.5 46.3 all-gather.1
  80.0 76.1 reduce-scatter.1
where the time goes:
time: 195 us
  blocking collectives  110 us (56%)
  matrix products  32.8 us (17%)
  waiting for transfers between devices  20.3 us (10%)
  between operations  13.5 us (7%)
  other arithmetic  11.4 us (6%)
  local copies, waits for them, and re-layouts  6.49 us (3%)
    psum x1, blocking collectives, body(): lax.psum(jnp.dot(factor_mode2, factor_mode2.T, preferred_element_type=jnp...  72.5 us
    psum x1, blocking collectives, body(): lax.psum(jnp.dot(factor_mode3, factor_mode3.T, preferred_element_type=jnp...  23.6 us
    all_gather x1, waiting for transfers between devices, body(): full_two = lax.all_gather(factor_mode2, 'col', axis=1, tiled=True)  19.6 us
    dot_general x1, matrix products, body(): jnp.einsum('trab,trb->tra', contracted, mode2_rows.astype(jnp.float32), p...  16.7 us
    all_gather x1, blocking collectives, body(): full_three = lax.all_gather(factor_mode3, 'row', axis=1, tiled=True)  14.2 us
    dot_general x1, matrix products, body(): jnp.einsum('trc,tabc->trab', mode3_rows, tensor_tiles, preferred_element_...  12.1 us
    another operation x3, other arithmetic, body(): cholesky_factor = jnp.linalg.cholesky(system)  5.05 us
    another operation x2, other arithmetic, body(): lax.linalg.triangular_solve(cholesky_factor, middle, left_side=True, lowe...  4.32 us
  transfers between devices with their start and end apart: 2, of which 1 were waited for; matrix products, arithmetic and copies ran while one was open for 13% of the time, Pallas kernels for 0%

commit v1 on v0

v1 whole, which is shorter than its diff:
```python
import jax
import jax.numpy as jnp
from jax import lax
from jax.experimental import pallas as pl
from jax.experimental.pallas import tpu as pltpu
from jax.sharding import PartitionSpec as P

IB_DEV = 8
META = 8

ridge_term = 0.5

F32 = jnp.float32
BF16 = jnp.bfloat16
VMEM = pl.BlockSpec(memory_space=pltpu.VMEM)
SMEM = pl.BlockSpec(memory_space=pltpu.SMEM)
MIB = 1 << 20


def first_kernel(mode3_ref, three_ref, tiles_ref, out_ref, weight_ref):
    rank = three_ref.shape[1]
    edge = tiles_ref.shape[3]
    per_owner = three_ref.shape[2] // edge
    pair = pl.program_id(0)

    @pl.when(pl.program_id(1) == 0)
    def _():
        weight_ref[...] = jnp.zeros_like(weight_ref)
        for side in range(2):
            block = mode3_ref[2 * pair + side]
            start = pl.multiple_of(lax.rem(block, per_owner) * edge, edge)
            rows = three_ref[lax.div(block, per_owner), :, pl.ds(start, edge)]
            weight_ref[side * rank : (side + 1) * rank, side * edge : (side + 1) * edge] = rows

    both = jnp.concatenate([tiles_ref[0, 0], tiles_ref[0, 1]], axis=-1)
    out_ref[0] = lax.dot_general(
        both, weight_ref[...], (((1,), (1,)), ((), ())), preferred_element_type=F32
    )


def contract_first(mode3, three, tiles):
    tile_count, edge = tiles.shape[0], tiles.shape[1]
    pairs = tile_count // 2
    rows = edge * edge
    step = 4096
    tiles = tiles.reshape(pairs, 2, rows, edge)
    return pl.pallas_call(
        first_kernel,
        grid=(pairs, rows // step),
        in_specs=[
            SMEM,
            VMEM,
            pl.BlockSpec((1, 2, step, edge), lambda p, s: (p, 0, s, 0)),
        ],
        out_specs=pl.BlockSpec((1, step, 128), lambda p, s: (p, s, 0)),
        out_shape=jax.ShapeDtypeStruct((pairs, rows, 128), F32),
        scratch_shapes=[pltpu.VMEM((128, 2 * edge), BF16)],
        compiler_params=pltpu.CompilerParams(vmem_limit_bytes=14 * MIB),
        cost_estimate=pl.CostEstimate(
            flops=2 * pairs * rows * 256 * 256, bytes_accessed=40 * MIB, transcendentals=0
        ),
        name="contract_first",
    )(mode3, three, tiles)


def half_rows(own, other, first):
    low = jnp.where(first, own, other)
    high = jnp.where(first, other, own)
    return low, high


def second_kernel(mode1_ref, mode2_ref, core_ref, mid_ref, own_ref, other_ref, send_ref, row_ref):
    owners, half, width = own_ref.shape
    rank = 2 * half
    edge = send_ref.shape[2]
    per_owner = width // edge
    pairs = mid_ref.shape[0]
    first = core_ref[0] == 0
    send_ref[...] = jnp.zeros_like(send_ref)
    for pair in range(pairs):
        parts = []
        for side in range(2):
            block = mode2_ref[2 * pair + side]
            start = pl.multiple_of(lax.rem(block, per_owner) * edge, edge)
            owner = lax.div(block, per_owner)
            own = own_ref[owner, :, pl.ds(start, edge)].astype(F32)
            other = other_ref[owner, :, pl.ds(start, edge)].astype(F32)
            parts.extend(half_rows(own, other, first))
        parts.append(jnp.zeros((128 - 2 * rank, edge), F32))
        factor = jnp.concatenate(parts, axis=0).T.reshape(1, edge // 8, 8, 128)

        @pl.loop(0, edge // 8)
        def _(group):
            start = pl.multiple_of(group * 8 * edge, 8 * edge)
            block = mid_ref[pair, pl.ds(start, 8 * edge), :].reshape(8, edge // 8, 8, 128)
            summed = jnp.sum(block * factor, axis=1)
            row_ref[pl.ds(pl.multiple_of(group * 8, 8), 8), :] = jnp.sum(summed, axis=1)

        flipped = row_ref[...].T
        for side in range(2):
            block = mode1_ref[2 * pair + side]
            slot = lax.rem(lax.div(block, IB_DEV), owners)
            offset = lax.rem(block, IB_DEV).astype(F32)
            send_ref[slot, 0:rank, :] = flipped[side * rank : (side + 1) * rank, :]
            send_ref[slot, rank : rank + META, :] = jnp.full((META, edge), offset, F32)


def contract_second(mode1, mode2, core, mid, own, other):
    owners, half, _ = own.shape
    return pl.pallas_call(
        second_kernel,
        in_specs=[SMEM, SMEM, SMEM, VMEM, VMEM, VMEM],
        out_specs=VMEM,
        out_shape=jax.ShapeDtypeStruct((owners, 2 * half + META, 128), F32),
        scratch_shapes=[pltpu.VMEM((128, 128), F32)],
        compiler_params=pltpu.CompilerParams(vmem_limit_bytes=24 * MIB),
        cost_estimate=pl.CostEstimate(flops=8 * MIB, bytes_accessed=20 * MIB, transcendentals=0),
        name="contract_second",
    )(mode1, mode2, core, mid, own, other)


def inverse_kernel(core_ref, own_ref, other_ref, three_ref, out_ref):
    owners, half, _ = own_ref.shape
    rank = 2 * half
    first = core_ref[0] == 0
    contract = (((1,), (1,)), ((), ()))
    gram_two = jnp.zeros((rank, rank), F32)
    for owner in range(owners):
        low, high = half_rows(own_ref[owner].astype(F32), other_ref[owner].astype(F32), first)
        rows = jnp.concatenate([low, high], axis=0).astype(BF16)
        gram_two += lax.dot_general(rows, rows, contract, preferred_element_type=F32)
    gram_three = jnp.zeros((rank, rank), F32)
    for owner in range(three_ref.shape[0]):
        rows = three_ref[owner]
        gram_three += lax.dot_general(rows, rows, contract, preferred_element_type=F32)
    row_ids = lax.broadcasted_iota(jnp.int32, (rank, rank), 0)
    col_ids = lax.broadcasted_iota(jnp.int32, (rank, rank), 1)
    unit = (row_ids == col_ids).astype(F32)
    system = gram_two * gram_three + ridge_term * unit
    work = jnp.concatenate([system, unit, jnp.zeros((rank, 128 - 2 * rank), F32)], axis=1)
    below = lax.broadcasted_iota(jnp.int32, (rank, 128), 0)
    scale = jnp.zeros((rank, 128), F32)
    for k in range(rank):
        pivot_row = work[k : k + 1, :]
        inverse = 1.0 / pivot_row[:, k : k + 1]
        scale = jnp.where(below == k, inverse, scale)
        factor = jnp.where(below > k, work[:, k : k + 1] * inverse, 0.0)
        work = work - factor * pivot_row
    lower = work[:, rank : 2 * rank]
    out_ref[...] = lax.dot_general(
        lower,
        lower * scale[:, :rank],
        (((0,), (0,)), ((), ())),
        precision=lax.Precision.HIGHEST,
        preferred_element_type=F32,
    )


def system_inverse(core, own, other, three):
    rank = three.shape[1]
    return pl.pallas_call(
        inverse_kernel,
        in_specs=[SMEM, VMEM, VMEM, VMEM],
        out_specs=VMEM,
        out_shape=jax.ShapeDtypeStruct((rank, rank), F32),
        compiler_params=pltpu.CompilerParams(vmem_limit_bytes=16 * MIB),
        cost_estimate=pl.CostEstimate(flops=8 * MIB, bytes_accessed=16 * MIB, transcendentals=0),
        name="system_inverse",
    )(core, own, other, three)


def solve_kernel(received_ref, inverse_ref, out_ref, side_ref):
    owners, _, edge = received_ref.shape
    rank = inverse_ref.shape[0]
    for offset in range(IB_DEV):
        total = jnp.zeros((rank // 8, 8, edge), F32)
        for owner in range(owners):
            hit = (received_ref[owner, rank : rank + META, :] == float(offset))[None]
            rows = received_ref[owner, 0:rank, :].reshape(rank // 8, 8, edge)
            total += jnp.where(hit, rows, 0.0)
        side_ref[:, offset * edge : (offset + 1) * edge] = total.reshape(rank, edge)
    out_ref[...] = jnp.dot(
        inverse_ref[...],
        side_ref[...],
        precision=lax.Precision.HIGHEST,
        preferred_element_type=F32,
    )


def solve(received, inverse):
    rank = inverse.shape[0]
    edge = received.shape[2]
    return pl.pallas_call(
        solve_kernel,
        in_specs=[VMEM, VMEM],
        out_specs=VMEM,
        out_shape=jax.ShapeDtypeStruct((rank, IB_DEV * edge), F32),
        scratch_shapes=[pltpu.VMEM((rank, IB_DEV * edge), F32)],
        compiler_params=pltpu.CompilerParams(vmem_limit_bytes=16 * MIB),
        name="solve",
    )(received, inverse)


def body(tensor_tiles, tile_mode1, tile_mode2, tile_mode3, factor_mode2, factor_mode3):
    rank, width = factor_mode2.shape
    half = rank // 2
    cols = lax.axis_size("col")
    core = lax.rem(lax.axis_index("row"), 2).astype(jnp.int32)
    mine = lax.dynamic_slice_in_dim(factor_mode2, core * half, half, 0)
    own = lax.all_to_all(
        jnp.broadcast_to(mine[None], (cols, half, width)), "col", 0, 0, tiled=True
    )
    three = lax.all_gather(factor_mode3, "row", axis=0, tiled=False)
    mid = contract_first(tile_mode3, three, tensor_tiles)
    swap = [(i, i ^ 1) for i in range(lax.axis_size("row"))]
    other = lax.ppermute(own, "row", swap)
    core_id = core[None]
    send = contract_second(tile_mode1, tile_mode2, core_id, mid, own, other)
    received = lax.all_to_all(send, "col", 0, 0, tiled=True)
    inverse = system_inverse(core_id, own, other, three)
    return solve(received, inverse)


def solution(mesh):
    in_specs = (
        P(("row", "col"), None, None, None),
        P(("row", "col")),
        P(("row", "col")),
        P(("row", "col")),
        P(None, "col"),
        P(None, "row"),
    )
    out_specs = P(None, ("row", "col"))
    return jax.shard_map(body, mesh=mesh, in_specs=in_specs, out_specs=out_specs, check_vma=False)
```

time: 195 us -> 70.7 us (0.36)
  blocking collectives: 110 us -> 36.1 us
  matrix products: 32.8 us -> 0 us
  Pallas kernels: 0 us -> 16.8 us
  waiting for transfers between devices: 20.3 us -> 6.43 us
  between operations: 13.5 us -> 0.06 us
  other arithmetic: 11.4 us -> 0 us
  starting transfers between devices: 0.04 us -> 3.68 us
    psum x2 -> x0, blocking collectives: 96.1 us -> none  [the longest x1 72.5 us: body(): lax.psum(jnp.dot(factor_mode2, factor_mode2.T, preferred_element_type=jnp...]
    dot_general x5 -> x0, matrix products: 30.5 us -> none  [the longest x1 16.7 us: body(): jnp.einsum('trab,trb->tra', contracted, mode2_rows.astype(jnp.float32), p...]
    all_to_all x0 -> x1, blocking collectives: none -> 21.9 us  [body(): lax.all_to_all(jnp.broadcast_to(mine[None], (cols, half, width)), 'col',...]
    all_gather x1 -> x0, waiting for transfers between devices: 19.6 us -> none  [body(): full_two = lax.all_gather(factor_mode2, 'col', axis=1, tiled=True)]
    pallas_call x0 -> x4, Pallas kernels: none -> 16.8 us  [the longest x1 7.34 us: contract_first(): pl.pallas_call(first_kernel, grid=(pairs, rows // step), in_specs=[SMEM,...]
    another operation x5 -> x0, other arithmetic: 9.38 us -> none  [the longest x3 5.05 us: body(): cholesky_factor = jnp.linalg.cholesky(system)]
    all_to_all x0 -> x1, waiting for transfers between devices: none -> 6.43 us  [body(): received = lax.all_to_all(send, 'col', 0, 0, tiled=True)]
    unnamed x5 -> x10, local copies, waits for them, and re-layouts: 3.47 us -> 7.32 us
  transfers between devices with their start and end apart: 2 -> 2, of which waited for: 1 -> 1; matrix products, arithmetic and copies ran while one was open for 13% -> 0% of each run, Pallas kernels for 0% -> 18%
where the time goes in v1:
time: 70.7 us; the launch traced here: 70.4 us
  blocking collectives  36.1 us (51%)
  Pallas kernels  16.8 us (24%)
  local copies, waits for them, and re-layouts  7.41 us (10%)
  waiting for transfers between devices  6.43 us (9%)
  starting transfers between devices  3.68 us (5%)
    all_to_all x1, blocking collectives, body(): lax.all_to_all(jnp.broadcast_to(mine[None], (cols, half, width)), 'col',...  21.9 us
    all_gather x1, blocking collectives, body(): three = lax.all_gather(factor_mode3, 'row', axis=0, tiled=False)  14.2 us
    pallas_call x1, Pallas kernels, contract_first(): pl.pallas_call(first_kernel, grid=(pairs, rows // step), in_specs=[SMEM,...  7.34 us
    unnamed x10, local copies, waits for them, and re-layouts  7.32 us
    all_to_all x1, waiting for transfers between devices, body(): received = lax.all_to_all(send, 'col', 0, 0, tiled=True)  6.43 us
    pallas_call x1, Pallas kernels, system_inverse(): pl.pallas_call(inverse_kernel, in_specs=[SMEM, VMEM, VMEM, VMEM], out_spe...  5 us
    all_to_all x1, starting transfers between devices, body(): received = lax.all_to_all(send, 'col', 0, 0, tiled=True)  3.67 us
    pallas_call x1, Pallas kernels, contract_second(): pl.pallas_call(second_kernel, in_specs=[SMEM, SMEM, SMEM, VMEM, VMEM, VME...  3.25 us
  transfers between devices with their start and end apart: 2, of which 1 were waited for; matrix products, arithmetic and copies ran while one was open for 0% of the time, Pallas kernels for 18%

profile of v1, /device:TPU:0, one launch (start us, length us, event | category | flops | bytes accessed | tf_op | source)
XLA Modules:
  0.0 70.4 jit_solution(11183759379990555284)
XLA Ops:
  0.0 0.0 copy-start
  0.0 0.9 %copy-done = bf16[48,1024]{1,0:T(8,128)(2,1)S(1)} copy-done((bf16[48,1024]{1,0:T(8,128)(2,1)S(1)}, bf16[48,1024]{1,0:T(8,128)(2,1)}, u32[]{:S(2)}) %copy-start) | copy-done | bytes 98328
  0.9 0.1 broadcast_in_dim.10
  1.0 21.9 %all_to_all.10.own_ref = bf16[16,24,1024]{2,1,0:T(8,128)(2,1)S(1)} all-to-all(bf16[16,24,1024]{2,1,0:T(8,128)(2,1)S(1)} %broadcast_in_dim.10), channel_id=1, replica_groups=mesh['row'=8,'col'=16] {'col'}, dimensions={0} | all-to-all | bytes 1572864 | tf_op jit(solution)/shard_map/all_to_all | solution.py:210
  22.9 0.0 collective-permute-start
  22.9 14.2 %all-gather = bf16[384,1024]{1,0:T(8,128)(2,1)S(1)} all-gather(bf16[48,1024]{1,0:T(8,128)(2,1)} %param.11), channel_id=2, replica_groups=mesh['row'=8,'col'=16] {'row'}, dimensions={0}, use_global_device_ids=true | all-gather | bytes 884736 | tf_op jit(solution)/shard_map/all_gather | solution.py:213
  37.1 0.0 copy-start.1
  37.1 5.8 %copy-done.1 = bf16[4,128,128,128]{3,2,1,0:T(8,128)(2,1)S(1)} copy-done((bf16[4,128,128,128]{3,2,1,0:T(8,128)(2,1)S(1)}, bf16[4,128,128,128]{3,2,1,0:T(8,128)(2,1)}, u32[]{:S(2)}) %copy-start.1) | copy-done | bytes 16777240
  42.8 0.0 copy-start.2
  42.8 0.7 copy-done.2
  43.5 0.0 copy-start.3
  43.5 0.0 copy-start.4
  43.5 7.3 %contract_first.1.mid_ref = f32[2,16384,128]{2,1,0:T(8,128)S(1)} custom-call(s32[4]{0:T(128)S(1)} %copy-done.2, bf16[8,48,1024]{2,1,0:T(8,128)(2,1)S(1)} %bitcast.4, bf16[2,2,16384,128]{3,2,1,0:T(8,128)(2,1)S(1)} %bitcast.3), custom_call_target="tpu_custom_call" | custom-call | flops 4294967296 | bytes 41943040 | tf_op jit(solution)/shard_map/contract_first/pallas_call | solution.py:47
  50.8 0.0 collective-permute-done.other_ref
  50.9 0.0 copy-done.3
  50.9 0.0 copy-done.4
  50.9 3.2 %contract_second.1 = f32[16,56,128]{2,1,0:T(8,128)} custom-call(s32[4]{0:T(128)S(1)} %copy-done.3, s32[4]{0:T(128)S(1)} %copy-done.4, s32[1]{0:T(128)} %bitcast.core_ref, f32[2,16384,128]{2,1,0:T(8,128)S(1)} %contract_first.1.mid_ref, bf16[16,24,1024]{2,1,0:T(8,128)(2,1)S(1)} %all_to_all.10.own_ref, bf16[16,24,1024]{2,1,0:T(8,128)(2,1)S(1)} %collective-permute-done.other_ref), custom_call_target="tpu_custom_call" | custom-call | flops 8388608 | bytes 20971520 | tf_op jit(solution)/shard_map/contract_second/pallas_call | solution.py:110
  54.1 3.7 %all-to-all-start.1 = ((f32[16,56,128]{2,1,0:T(8,128)}), f32[16,56,128]{2,1,0:T(8,128)S(1)}, u32[]{:S(2)}, u32[]{:S(2)}) async-start(f32[16,56,128]{2,1,0:T(8,128)} %contract_second.1), calls=%async_computation.1 | async-start | bytes 917504 | tf_op jit(solution)/shard_map/all_to_all | solution.py:219
  57.8 5.0 %system_inverse.1.inverse_ref = f32[48,48]{1,0:T(8,128)S(1)} custom-call(s32[1]{0:T(128)} %bitcast.core_ref, bf16[16,24,1024]{2,1,0:T(8,128)(2,1)S(1)} %all_to_all.10.own_ref, bf16[16,24,1024]{2,1,0:T(8,128)(2,1)S(1)} %collective-permute-done.other_ref, bf16[8,48,1024]{2,1,0:T(8,128)(2,1)S(1)} %bitcast.5), custom_call_target="tpu_custom_call" | custom-call | flops 8388608 | bytes 16777216 | tf_op jit(solution)/shard_map/system_inverse/pallas_call | solution.py:161
  62.8 6.4 %all-to-all-done.1.received_ref = f32[16,56,128]{2,1,0:T(8,128)S(1)} async-done(((f32[16,56,128]{2,1,0:T(8,128)}), f32[16,56,128]{2,1,0:T(8,128)S(1)}, u32[]{:S(2)}, u32[]{:S(2)}) %all-to-all-start.1) | async-done | bytes 458784 | tf_op jit(solution)/shard_map/all_to_all | solution.py:219
  69.2 1.2 %solve.1 = f32[48,1024]{1,0:T(8,128)} custom-call(f32[16,56,128]{2,1,0:T(8,128)S(1)} %all-to-all-done.1.received_ref, f32[48,48]{1,0:T(8,128)S(1)} %system_inverse.1.inverse_ref), custom_call_target="tpu_custom_call" | custom-call | tf_op jit(solution)/shard_map/solve/pallas_call | solution.py:193
  (1 shorter events, 0.0 us)
Async XLA Ops:
  0.0 0.9 %copy-start = (bf16[48,1024]{1,0:T(8,128)(2,1)S(1)}, bf16[48,1024]{1,0:T(8,128)(2,1)}, u32[]{:S(2)}) copy-start(bf16[48,1024]{1,0:T(8,128)(2,1)} %param.10) | copy-start | bytes 294916
  22.9 27.9 %collective-permute-start = (bf16[16,24,1024]{2,1,0:T(8,128)(2,1)S(1)}, bf16[16,24,1024]{2,1,0:T(8,128)(2,1)S(1)}, u32[]{:S(2)}, u32[]{:S(2)}) collective-permute-start(bf16[16,24,1024]{2,1,0:T(8,128)(2,1)S(1)} %all_to_all.10.own_ref), channel_id=1, source_target_pairs={{0,16},{16,0},{32,48},{48,32},{64,80},{80,64},{96,112},{112,96},{1... | collective-permute-start | bytes 2359304 | tf_op jit(solution)/shard_map/ppermute | solution.py:216
  37.1 5.8 %copy-start.1 = (bf16[4,128,128,128]{3,2,1,0:T(8,128)(2,1)S(1)}, bf16[4,128,128,128]{3,2,1,0:T(8,128)(2,1)}, u32[]{:S(2)}) copy-start(bf16[4,128,128,128]{3,2,1,0:T(8,128)(2,1)} %param.6) | copy-start | bytes 50331652
  42.8 0.7 copy-start.2
  43.5 7.4 %copy-start.3 = (s32[4]{0:T(128)S(1)}, s32[4]{0:T(128)}, u32[]{:S(2)}) copy-start(s32[4]{0:T(128)} %mode1_ref.1) | copy-start | bytes 52
  43.5 7.4 %copy-start.4 = (s32[4]{0:T(128)S(1)}, s32[4]{0:T(128)}, u32[]{:S(2)}) copy-start(s32[4]{0:T(128)} %mode2_ref.1) | copy-start | bytes 52
  54.1 15.1 %all-to-all-start.1 = ((f32[16,56,128]{2,1,0:T(8,128)}), f32[16,56,128]{2,1,0:T(8,128)S(1)}, u32[]{:S(2)}, u32[]{:S(2)}) async-start(f32[16,56,128]{2,1,0:T(8,128)} %contract_second.1), calls=%async_computation.1 | async-start | bytes 917504 | tf_op jit(solution)/shard_map/all_to_all | solution.py:219

commit v2 on v1

v2 whole, which is shorter than its diff:
```python
import jax
import jax.numpy as jnp
from jax import lax
from jax.experimental import pallas as pl
from jax.experimental.pallas import tpu as pltpu
from jax.sharding import PartitionSpec as P


IB_DEV = 8
META = 8

ridge_term = 0.5

F32 = jnp.float32
BF16 = jnp.bfloat16
VMEM = pl.BlockSpec(memory_space=pltpu.VMEM)
HBM = pl.BlockSpec(memory_space=pltpu.HBM)
SMEM = pl.BlockSpec(memory_space=pltpu.SMEM)
MIB = 1 << 20


CHUNKS = 4
EARLY = 2
DEPTH = 3
PARTS = 2


def early_kernel(tiles_ref, out_ref, sems):
    step = out_ref.shape[2]
    copies = [
        pltpu.make_async_copy(
            tiles_ref.at[side, pl.ds(chunk * step, step)],
            out_ref.at[side, chunk],
            sems.at[side, chunk],
        )
        for chunk in range(EARLY)
        for side in range(2)
    ]
    for copy in copies:
        copy.start()
    for copy in copies:
        copy.wait()


def fetch_early(tiles):
    edge = tiles.shape[1]
    return pl.pallas_call(
        early_kernel,
        in_specs=[HBM],
        out_specs=VMEM,
        out_shape=jax.ShapeDtypeStruct((2, EARLY, edge // CHUNKS, edge, edge), BF16),
        scratch_shapes=[pltpu.SemaphoreType.DMA((2, EARLY))],
        compiler_params=pltpu.CompilerParams(vmem_limit_bytes=8 * MIB),
        cost_estimate=pl.CostEstimate(flops=0, bytes_accessed=8 * MIB, transcendentals=0),
        name="fetch_early",
    )(tiles)


def half_rows(own, other, first):
    low = jnp.where(first, own, other)
    high = jnp.where(first, other, own)
    return low, high


def near_slot(row, owner, chips):
    distance = lax.rem(lax.div(row, 2) - lax.div(owner, 2) + chips, chips)
    return distance + chips * lax.rem(row + owner, 2)


def rows_kernel(
    mode1_ref,
    mode2_ref,
    mode3_ref,
    row_id_ref,
    own_ref,
    other_ref,
    three_ref,
    early_ref,
    tiles_ref,
    send_ref,
    weight_ref,
    tile_ref,
    row_ref,
    sems,
):
    tile_count, edge = tiles_ref.shape[:2]
    step = edge // CHUNKS
    steps = [(pair, chunk) for pair in range(tile_count // 2) for chunk in range(CHUNKS)]
    late = steps[EARLY:]

    def copies(number):
        pair, chunk = late[number]
        return [
            pltpu.make_async_copy(
                tiles_ref.at[2 * pair + side, pl.ds(chunk * step, step)],
                tile_ref.at[number, side],
                sems.at[number, side],
            )
            for side in range(2)
        ]

    for number in range(DEPTH):
        for copy in copies(number):
            copy.start()

    @pl.when(row_id_ref[0] >= 0)
    def _():
        fill_rows(
            mode1_ref,
            mode2_ref,
            mode3_ref,
            row_id_ref,
            own_ref,
            other_ref,
            three_ref,
            early_ref,
            send_ref,
            weight_ref,
            tile_ref,
            row_ref,
            steps,
            late,
            copies,
        )


def fill_rows(
    mode1_ref,
    mode2_ref,
    mode3_ref,
    row_id_ref,
    own_ref,
    other_ref,
    three_ref,
    early_ref,
    send_ref,
    weight_ref,
    tile_ref,
    row_ref,
    steps,
    late,
    copies,
):
    owners, half, width = own_ref.shape
    rank = 2 * half
    edge = tile_ref.shape[-1]
    step = tile_ref.shape[2]
    pairs = weight_ref.shape[0]
    per_owner = width // edge

    def place(block):
        start = pl.multiple_of(lax.rem(block, per_owner) * edge, edge)
        return lax.div(block, per_owner), pl.ds(start, edge)

    first = lax.rem(row_id_ref[0], 2) == 0
    send_ref[...] = jnp.zeros_like(send_ref)
    weight_ref[...] = jnp.zeros_like(weight_ref)
    factors = []
    for pair in range(pairs):
        parts = []
        for side in range(2):
            owner, span = place(mode3_ref[2 * pair + side])
            owner = near_slot(row_id_ref[0], owner, three_ref.shape[0] // 2)
            weight_ref[pair, side * rank : (side + 1) * rank, side * edge : (side + 1) * edge] = (
                three_ref[owner, :, span]
            )
            owner, span = place(mode2_ref[2 * pair + side])
            own = own_ref[owner, :, span].astype(F32)
            other = other_ref[owner, :, span].astype(F32)
            parts.extend(half_rows(own, other, first))
        parts.append(jnp.zeros((128 - 2 * rank, edge), F32))
        factors.append(jnp.concatenate(parts, axis=0).T.reshape(1, edge // 8, 8, 128))

    part = step // PARTS
    for number, (pair, chunk) in enumerate(steps):
        if number >= EARLY:
            late_number = number - EARLY
            for copy in copies(late_number):
                copy.wait()
            if late_number + DEPTH < len(late):
                for copy in copies(late_number + DEPTH):
                    copy.start()
        for index in range(PARTS):
            inner = slice(index * part, (index + 1) * part)
            if number < EARLY:
                sides = [early_ref[side, chunk, inner] for side in range(2)]
            else:
                sides = [tile_ref[late_number, side, inner] for side in range(2)]
            both = jnp.concatenate(sides, axis=-1).reshape(part * edge, 2 * edge)
            mid = lax.dot_general(
                both, weight_ref[pair], (((1,), (1,)), ((), ())), preferred_element_type=F32
            )
            terms = mid.reshape(part, edge // 8, 8, 128) * factors[pair]
            while terms.shape[1] > 1:
                terms = terms.reshape(part, terms.shape[1] // 2, 2, 8, 128)
                terms = terms[:, :, 0] + terms[:, :, 1]
            start = chunk * step + index * part
            row_ref[start : start + part, :] = jnp.sum(terms.reshape(part, 8, 128), axis=1)
        if chunk == CHUNKS - 1:
            flipped = row_ref[...].T
            for side in range(2):
                block = mode1_ref[2 * pair + side]
                slot = lax.rem(lax.div(block, IB_DEV), owners)
                offset = lax.rem(block, IB_DEV).astype(F32)
                send_ref[slot, 0:rank, :] = flipped[side * rank : (side + 1) * rank, :]
                send_ref[slot, rank : rank + META, :] = jnp.full((META, edge), offset, F32)


def tile_rows(mode1, mode2, mode3, row, own, other, three, early, tiles):
    owners, half, _ = own.shape
    tile_count, edge = tiles.shape[:2]
    late = tile_count // 2 * CHUNKS - EARLY
    return pl.pallas_call(
        rows_kernel,
        in_specs=[SMEM] * 4 + [VMEM] * 4 + [HBM],
        out_specs=VMEM,
        out_shape=jax.ShapeDtypeStruct((owners, 2 * half + META, edge), F32),
        scratch_shapes=[
            pltpu.VMEM((tile_count // 2, 128, 2 * edge), BF16),
            pltpu.VMEM((late, 2, edge // CHUNKS, edge, edge), BF16),
            pltpu.VMEM((edge, 128), F32),
            pltpu.SemaphoreType.DMA((late, 2)),
        ],
        compiler_params=pltpu.CompilerParams(vmem_limit_bytes=32 * MIB),
        cost_estimate=pl.CostEstimate(
            flops=tile_count * edge * edge * 256 * 256, bytes_accessed=16 * MIB, transcendentals=0
        ),
        name="tile_rows",
    )(mode1, mode2, mode3, row, own, other, three, early, tiles)


def inverse_kernel(row_id_ref, own_ref, other_ref, three_ref, out_ref):
    owners, half, _ = own_ref.shape
    rank = 2 * half
    first = lax.rem(row_id_ref[0], 2) == 0
    contract = (((1,), (1,)), ((), ()))
    gram_two = jnp.zeros((rank, rank), F32)
    for owner in range(owners):
        low, high = half_rows(own_ref[owner].astype(F32), other_ref[owner].astype(F32), first)
        rows = jnp.concatenate([low, high], axis=0).astype(BF16)
        gram_two += lax.dot_general(rows, rows, contract, preferred_element_type=F32)
    gram_three = jnp.zeros((rank, rank), F32)
    for owner in range(three_ref.shape[0]):
        rows = three_ref[owner]
        gram_three += lax.dot_general(rows, rows, contract, preferred_element_type=F32)
    row_ids = lax.broadcasted_iota(jnp.int32, (rank, rank), 0)
    col_ids = lax.broadcasted_iota(jnp.int32, (rank, rank), 1)
    unit = (row_ids == col_ids).astype(F32)
    system = gram_two * gram_three + ridge_term * unit
    work = jnp.concatenate([system, unit, jnp.zeros((rank, 128 - 2 * rank), F32)], axis=1)
    below = lax.broadcasted_iota(jnp.int32, (rank, 128), 0)
    scale = jnp.zeros((rank, 128), F32)
    for k in range(rank):
        pivot_row = work[k : k + 1, :]
        inverse = 1.0 / pivot_row[:, k : k + 1]
        scale = jnp.where(below == k, inverse, scale)
        factor = jnp.where(below > k, work[:, k : k + 1] * inverse, 0.0)
        work = work - factor * pivot_row
    lower = work[:, rank : 2 * rank]
    out_ref[...] = lax.dot_general(
        lower,
        lower * scale[:, :rank],
        (((0,), (0,)), ((), ())),
        precision=lax.Precision.HIGHEST,
        preferred_element_type=F32,
    )


def system_inverse(row, own, other, three):
    rank = three.shape[1]
    return pl.pallas_call(
        inverse_kernel,
        in_specs=[SMEM, VMEM, VMEM, VMEM],
        out_specs=VMEM,
        out_shape=jax.ShapeDtypeStruct((rank, rank), F32),
        compiler_params=pltpu.CompilerParams(vmem_limit_bytes=16 * MIB),
        cost_estimate=pl.CostEstimate(flops=8 * MIB, bytes_accessed=16 * MIB, transcendentals=0),
        name="system_inverse",
    )(row, own, other, three)


def solve_kernel(received_ref, inverse_ref, out_ref, side_ref):
    owners, _, edge = received_ref.shape
    rank = inverse_ref.shape[0]
    for offset in range(IB_DEV):
        total = jnp.zeros((rank // 8, 8, edge), F32)
        for owner in range(owners):
            hit = (received_ref[owner, rank : rank + META, :] == float(offset))[None]
            rows = received_ref[owner, 0:rank, :].reshape(rank // 8, 8, edge)
            total += jnp.where(hit, rows, 0.0)
        side_ref[:, offset * edge : (offset + 1) * edge] = total.reshape(rank, edge)
    out_ref[...] = jnp.dot(
        inverse_ref[...],
        side_ref[...],
        precision=lax.Precision.HIGHEST,
        preferred_element_type=F32,
    )


def solve(received, inverse):
    rank = inverse.shape[0]
    edge = received.shape[2]
    return pl.pallas_call(
        solve_kernel,
        in_specs=[VMEM, VMEM],
        out_specs=VMEM,
        out_shape=jax.ShapeDtypeStruct((rank, IB_DEV * edge), F32),
        scratch_shapes=[pltpu.VMEM((rank, IB_DEV * edge), F32)],
        compiler_params=pltpu.CompilerParams(vmem_limit_bytes=16 * MIB),
        name="solve",
    )(received, inverse)


def update(tensor_tiles, tile_mode1, tile_mode2, tile_mode3, factor_mode2, factor_mode3):
    rank, width = factor_mode2.shape
    half = rank // 2
    cols = lax.axis_size("col")
    row = lax.axis_index("row").astype(jnp.int32)
    core = lax.rem(row, 2)
    mine = jnp.where(core == 0, factor_mode2[:half], factor_mode2[half:])
    tiles = pltpu.with_memory_space_constraint(tensor_tiles, pltpu.HBM)
    own = lax.all_to_all(jnp.broadcast_to(mine[None], (cols, half, width)), "col", 0, 0, tiled=True)
    devices = lax.axis_size("row")
    chips = devices // 2
    near, far = [factor_mode3], []
    for distance in range(1, chips):
        shift = [(i, (i + 2 * distance) % devices) for i in range(devices)]
        near.append(lax.ppermute(factor_mode3, "row", shift))
    for distance in range(chips):
        swap = [(i, i ^ 1) for i in range(devices)]
        far.append(lax.ppermute(near[distance], "row", swap))
    three = jnp.stack(near + far)
    swap = [(i, i ^ 1) for i in range(lax.axis_size("row"))]
    other = lax.ppermute(own, "row", swap)
    early = fetch_early(tiles)
    row_id = row[None]
    send = tile_rows(tile_mode1, tile_mode2, tile_mode3, row_id, own, other, three, early, tiles)
    received = lax.all_to_all(send, "col", 0, 0, tiled=True)
    inverse = system_inverse(row_id, own, other, three)
    return solve(received, inverse)


def solution(mesh):
    in_specs = (
        P(("row", "col"), None, None, None),
        P(("row", "col")),
        P(("row", "col")),
        P(("row", "col")),
        P(None, "col"),
        P(None, "row"),
    )
    out_specs = P(None, ("row", "col"))
    return jax.shard_map(update, mesh=mesh, in_specs=in_specs, out_specs=out_specs, check_vma=False)
```

time: 70.7 us -> 59.4 us (0.84)
  blocking collectives: 36.1 us -> 0 us
  starting transfers between devices: 3.68 us -> 18.2 us
  waiting for transfers between devices: 6.43 us -> 17.9 us
  local copies, waits for them, and re-layouts: 7.41 us -> 6.1 us
  Pallas kernels: 16.8 us -> 15.8 us
  other arithmetic: 0 us -> 0.83 us
    all_to_all x1 -> x0, blocking collectives: 21.9 us -> none  [body(): lax.all_to_all(jnp.broadcast_to(mine[None], (cols, half, width)), 'col',...]
    all_gather x1 -> x0, blocking collectives: 14.2 us -> none  [body(): three = lax.all_gather(factor_mode3, 'row', axis=0, tiled=False)]
    all_to_all x1 -> x2, waiting for transfers between devices: 6.43 us -> 15.7 us  [the longest x1 9.42 us: update(): lax.all_to_all(jnp.broadcast_to(mine[None], (cols, half, width)), 'col',...]
    all_to_all x1 -> x2, starting transfers between devices: 3.67 us -> 11.5 us  [the longest x1 7.88 us: update(): lax.all_to_all(jnp.broadcast_to(mine[None], (cols, half, width)), 'col',...]
    ppermute x1 -> x8, starting transfers between devices: 0.01 us -> 6.75 us  [the longest x3 6.01 us: update(): near.append(lax.ppermute(factor_mode3, 'row', shift))]
    unnamed x10 -> x17, local copies, waits for them, and re-layouts: 7.32 us -> 5.1 us
    ppermute x1 -> x8, waiting for transfers between devices: 0.01 us -> 2.2 us  [the longest x1 2.19 us: update(): other = lax.ppermute(own, 'row', swap)]
    pallas_call x2, Pallas kernels: 10.6 us -> 9.63 us  [the longest x1 7.43 us: tile_rows(): pl.pallas_call(rows_kernel, in_specs=[SMEM] * 4 + [VMEM] * 4 + [HBM], out...]
  transfers between devices with their start and end apart: 2 -> 10, of which waited for: 1 -> 3; matrix products, arithmetic and copies ran while one was open for 0% -> 5% of each run, Pallas kernels for 18% -> 12%
where the time goes in v2:
time: 59.4 us; the launch traced here: 59 us
  starting transfers between devices  18.2 us (31%)
  waiting for transfers between devices  17.9 us (30%)
  Pallas kernels  15.8 us (27%)
  local copies, waits for them, and re-layouts  6.1 us (10%)
  other arithmetic  0.83 us (1%)
    all_to_all x1, waiting for transfers between devices, update(): lax.all_to_all(jnp.broadcast_to(mine[None], (cols, half, width)), 'col',...  9.42 us
    all_to_all x1, starting transfers between devices, update(): lax.all_to_all(jnp.broadcast_to(mine[None], (cols, half, width)), 'col',...  7.88 us
    pallas_call x1, Pallas kernels, tile_rows(): pl.pallas_call(rows_kernel, in_specs=[SMEM] * 4 + [VMEM] * 4 + [HBM], out...  7.43 us
    all_to_all x1, waiting for transfers between devices, update(): received = lax.all_to_all(send, 'col', 0, 0, tiled=True)  6.29 us
    ppermute x3, starting transfers between devices, update(): near.append(lax.ppermute(factor_mode3, 'row', shift))  6.01 us
    unnamed x17, local copies, waits for them, and re-layouts  5.1 us
    pallas_call x1, Pallas kernels, system_inverse(): pl.pallas_call(inverse_kernel, in_specs=[SMEM, VMEM, VMEM, VMEM], out_spe...  5.01 us
    all_to_all x1, starting transfers between devices, update(): received = lax.all_to_all(send, 'col', 0, 0, tiled=True)  3.59 us
  transfers between devices with their start and end apart: 10, of which 3 were waited for; matrix products, arithmetic and copies ran while one was open for 5% of the time, Pallas kernels for 12%

profile of v2, /device:TPU:0, one launch (start us, length us, event | category | flops | bytes accessed | tf_op | source)
XLA Modules:
  0.0 59.0 jit_solution(15216254149079397956)
XLA Ops:
  0.0 1.8 %collective-permute-start.1 = (bf16[48,1024]{1,0:T(8,128)(2,1)}, bf16[48,1024]{1,0:T(8,128)(2,1)S(1)}, u32[]{:S(2)}, u32[]{:S(2)}) collective-permute-start(bf16[48,1024]{1,0:T(8,128)(2,1)} %param.11), channel_id=1, source_target_pairs={{0,32},{16,48},{32,64},{48,80},{64,96},{80,112},{96,0},{112,16},{1... | collective-permute-start | bytes 294920 | tf_op jit(solution)/shard_map/ppermute | solution.py:328
  1.8 2.9 %collective-permute-start.2 = (bf16[48,1024]{1,0:T(8,128)(2,1)}, bf16[48,1024]{1,0:T(8,128)(2,1)S(1)}, u32[]{:S(2)}, u32[]{:S(2)}) collective-permute-start(bf16[48,1024]{1,0:T(8,128)(2,1)} %param.11), channel_id=1, source_target_pairs={{0,64},{16,80},{32,96},{48,112},{64,0},{80,16},{96,32},{112,48},{1... | collective-permute-start | bytes 294920 | tf_op jit(solution)/shard_map/ppermute | solution.py:328
  4.7 1.3 %collective-permute-start.3 = (bf16[48,1024]{1,0:T(8,128)(2,1)}, bf16[48,1024]{1,0:T(8,128)(2,1)S(1)}, u32[]{:S(2)}, u32[]{:S(2)}) collective-permute-start(bf16[48,1024]{1,0:T(8,128)(2,1)} %param.11), channel_id=1, source_target_pairs={{0,96},{16,112},{32,0},{48,16},{64,32},{80,48},{96,64},{112,80},{1... | collective-permute-start | bytes 294920 | tf_op jit(solution)/shard_map/ppermute | solution.py:328
  6.0 0.0 collective-permute-start.4
  6.0 0.8 %slice_select_fusion = bf16[24,1024]{1,0:T(8,128)(2,1)S(1)} fusion(bf16[48,1024]{1,0:T(8,128)(2,1)} %param.10, pred[]{:T(512)S(6)} %eq.3), kind=kLoop, calls=%fused_computation.8 | loop fusion | flops 24576 | bytes 147457 | tf_op jit(solution)/shard_map/jit(_where)/select_n | solution.py:320
  6.9 1.0 %broadcast_in_dim.10 = bf16[16,24,1024]{2,1,0:T(8,128)(2,1)} broadcast(bf16[24,1024]{1,0:T(8,128)(2,1)S(1)} %slice_select_fusion), dimensions={1,2} | broadcast | bytes 835584 | tf_op jit(solution)/shard_map/broadcast_in_dim | solution.py:322
  7.8 7.9 %all-to-all-start = ((bf16[16,24,1024]{2,1,0:T(8,128)(2,1)}), bf16[16,24,1024]{2,1,0:T(8,128)(2,1)S(1)}, u32[]{:S(2)}, u32[]{:S(2)}) async-start(bf16[16,24,1024]{2,1,0:T(8,128)(2,1)} %broadcast_in_dim.10), calls=%async_computation | async-start | bytes 1572864 | tf_op jit(solution)/shard_map/all_to_all | solution.py:322
  15.7 0.9 %bitcast_dynamic-update-slice_fusion.7 = bf16[8,48,1024]{2,1,0:T(8,128)(2,1)S(1)} fusion(bf16[48,1024]{1,0:T(8,128)(2,1)} %param.11), kind=kLoop, calls=%fused_computation.7 | loop fusion | bytes 196608
  16.6 2.2 %fetch_early.1.early_ref = bf16[2,2,32,128,128]{4,3,2,1,0:T(8,128)(2,1)S(1)} custom-call(bf16[4,128,128,128]{3,2,1,0:T(8,128)(2,1)} %tiles_ref.3), custom_call_target="tpu_custom_call" | custom-call | bytes 8388608 | tf_op jit(solution)/shard_map/fetch_early/pallas_call | solution.py:47
  18.8 0.0 copy-start
  18.8 2.0 %copy-done = bf16[2,2,32,128,128]{4,3,2,1,0:T(8,128)(2,1)} copy-done((bf16[2,2,32,128,128]{4,3,2,1,0:T(8,128)(2,1)}, bf16[2,2,32,128,128]{4,3,2,1,0:T(8,128)(2,1)S(1)}, u32[]{:S(2)}) %copy-start) | copy-done | bytes 4194328
  20.8 0.0 collective-permute-done.1
  20.8 0.2 collective-permute-start.5
  21.0 0.0 collective-permute-done.2
  21.0 0.3 collective-permute-start.6
  21.3 0.0 collective-permute-done.3
  21.3 0.2 collective-permute-start.7
  21.6 9.4 %all-to-all-done.own_ref = bf16[16,24,1024]{2,1,0:T(8,128)(2,1)S(1)} async-done(((bf16[16,24,1024]{2,1,0:T(8,128)(2,1)}), bf16[16,24,1024]{2,1,0:T(8,128)(2,1)S(1)}, u32[]{:S(2)}, u32[]{:S(2)}) %all-to-all-start) | async-done | bytes 786464 | tf_op jit(solution)/shard_map/all_to_all | solution.py:322
  31.0 0.0 collective-permute-start
  31.0 0.0 collective-permute-done.4
  31.0 0.0 collective-permute-done.5
  31.1 0.0 collective-permute-done.6
  31.1 0.0 collective-permute-done.7
  31.1 2.2 %collective-permute-done.other_ref = bf16[16,24,1024]{2,1,0:T(8,128)(2,1)S(1)} collective-permute-done((bf16[16,24,1024]{2,1,0:T(8,128)(2,1)S(1)}, bf16[16,24,1024]{2,1,0:T(8,128)(2,1)S(1)}, u32[]{:S(2)}, u32[]{:S(2)}) %collective-permute-start) | collective-permute-done | bytes 786464 | tf_op jit(solution)/shard_map/ppermute | solution.py:334
  33.3 0.0 copy-done.2
  33.3 0.0 copy-done.3
  33.3 2.2 %copy-done.1 = bf16[2,2,32,128,128]{4,3,2,1,0:T(8,128)(2,1)S(1)} copy-done((bf16[2,2,32,128,128]{4,3,2,1,0:T(8,128)(2,1)S(1)}, bf16[2,2,32,128,128]{4,3,2,1,0:T(8,128)(2,1)}, u32[]{:S(2)}) %copy-start.1) | copy-done | bytes 4194328
  35.5 7.4 %tile_rows.1 = f32[16,56,128]{2,1,0:T(8,128)} custom-call(s32[4]{0:T(128)S(1)} %copy-done.2, s32[4]{0:T(128)S(1)} %copy-done.3, s32[4]{0:T(128)S(1)} %copy-done.4, s32[1]{0:T(128)} %bitcast.row_id_ref, bf16[16,24,1024]{2,1,0:T(8,128)(2,1)S(1)} %all-to-all-done.own_ref, bf16[16,24,1024]{2,1,0:T(8,128)(2,1)S(1)} %collective-permute-done.other_ref, ...), custom_call_target="tpu_custom_call" | custom-call | flops 4294967296 | bytes 16777216 | tf_op jit(solution)/shard_map/tile_rows/pallas_call | solution.py:213
  42.9 3.6 %all-to-all-start.1 = ((f32[16,56,128]{2,1,0:T(8,128)}), f32[16,56,128]{2,1,0:T(8,128)S(1)}, u32[]{:S(2)}, u32[]{:S(2)}) async-start(f32[16,56,128]{2,1,0:T(8,128)} %tile_rows.1), calls=%async_computation.1 | async-start | bytes 917504 | tf_op jit(solution)/shard_map/all_to_all | solution.py:338
  46.5 5.0 %system_inverse.1.inverse_ref = f32[48,48]{1,0:T(8,128)S(1)} custom-call(s32[1]{0:T(128)} %bitcast.row_id_ref, bf16[16,24,1024]{2,1,0:T(8,128)(2,1)S(1)} %all-to-all-done.own_ref, bf16[16,24,1024]{2,1,0:T(8,128)(2,1)S(1)} %collective-permute-done.other_ref, bf16[8,48,1024]{2,1,0:T(8,128)(2,1)S(1)} %bitcast_dynamic-update-slice_fusion.three_ref), custom_call_target="tpu_custom_call" | custom-call | flops 8388608 | bytes 16777216 | tf_op jit(solution)/shard_map/system_inverse/pallas_call | solution.py:271
  51.5 6.3 %all-to-all-done.1.received_ref = f32[16,56,128]{2,1,0:T(8,128)S(1)} async-done(((f32[16,56,128]{2,1,0:T(8,128)}), f32[16,56,128]{2,1,0:T(8,128)S(1)}, u32[]{:S(2)}, u32[]{:S(2)}) %all-to-all-start.1) | async-done | bytes 458784 | tf_op jit(solution)/shard_map/all_to_all | solution.py:338
  57.8 1.2 %solve.1 = f32[48,1024]{1,0:T(8,128)} custom-call(f32[16,56,128]{2,1,0:T(8,128)S(1)} %all-to-all-done.1.received_ref, f32[48,48]{1,0:T(8,128)S(1)} %system_inverse.1.inverse_ref), custom_call_target="tpu_custom_call" | custom-call | tf_op jit(solution)/shard_map/solve/pallas_call | solution.py:303
  (12 shorter events, 0.1 us)
Async XLA Ops:
  0.0 33.3 %copy-start.2 = (s32[4]{0:T(128)S(1)}, s32[4]{0:T(128)}, u32[]{:S(2)}) copy-start(s32[4]{0:T(128)} %mode1_ref.1) | copy-start | bytes 52
  0.0 33.3 %copy-start.3 = (s32[4]{0:T(128)S(1)}, s32[4]{0:T(128)}, u32[]{:S(2)}) copy-start(s32[4]{0:T(128)} %mode2_ref.1) | copy-start | bytes 52
  0.0 33.3 %copy-start.4 = (s32[4]{0:T(128)S(1)}, s32[4]{0:T(128)}, u32[]{:S(2)}) copy-start(s32[4]{0:T(128)} %mode3_ref.1) | copy-start | bytes 52
  0.0 20.8 %collective-permute-start.1 = (bf16[48,1024]{1,0:T(8,128)(2,1)}, bf16[48,1024]{1,0:T(8,128)(2,1)S(1)}, u32[]{:S(2)}, u32[]{:S(2)}) collective-permute-start(bf16[48,1024]{1,0:T(8,128)(2,1)} %param.11), channel_id=1, source_target_pairs={{0,32},{16,48},{32,64},{48,80},{64,96},{80,112},{96,0},{112,16},{1... | collective-permute-start | bytes 294920 | tf_op jit(solution)/shard_map/ppermute | solution.py:328
  1.8 19.3 %collective-permute-start.2 = (bf16[48,1024]{1,0:T(8,128)(2,1)}, bf16[48,1024]{1,0:T(8,128)(2,1)S(1)}, u32[]{:S(2)}, u32[]{:S(2)}) collective-permute-start(bf16[48,1024]{1,0:T(8,128)(2,1)} %param.11), channel_id=1, source_target_pairs={{0,64},{16,80},{32,96},{48,112},{64,0},{80,16},{96,32},{112,48},{1... | collective-permute-start | bytes 294920 | tf_op jit(solution)/shard_map/ppermute | solution.py:328
  4.7 16.7 %collective-permute-start.3 = (bf16[48,1024]{1,0:T(8,128)(2,1)}, bf16[48,1024]{1,0:T(8,128)(2,1)S(1)}, u32[]{:S(2)}, u32[]{:S(2)}) collective-permute-start(bf16[48,1024]{1,0:T(8,128)(2,1)} %param.11), channel_id=1, source_target_pairs={{0,96},{16,112},{32,0},{48,16},{64,32},{80,48},{96,64},{112,80},{1... | collective-permute-start | bytes 294920 | tf_op jit(solution)/shard_map/ppermute | solution.py:328
  6.0 25.0 %collective-permute-start.4 = (bf16[48,1024]{1,0:T(8,128)(2,1)}, bf16[48,1024]{1,0:T(8,128)(2,1)S(1)}, u32[]{:S(2)}, u32[]{:S(2)}) collective-permute-start(bf16[48,1024]{1,0:T(8,128)(2,1)} %param.11), channel_id=1, source_target_pairs={{0,16},{16,0},{32,48},{48,32},{64,80},{80,64},{96,112},{112,96},{1... | collective-permute-start | bytes 294920 | tf_op jit(solution)/shard_map/ppermute | solution.py:331
  7.8 23.2 %all-to-all-start = ((bf16[16,24,1024]{2,1,0:T(8,128)(2,1)}), bf16[16,24,1024]{2,1,0:T(8,128)(2,1)S(1)}, u32[]{:S(2)}, u32[]{:S(2)}) async-start(bf16[16,24,1024]{2,1,0:T(8,128)(2,1)} %broadcast_in_dim.10), calls=%async_computation | async-start | bytes 1572864 | tf_op jit(solution)/shard_map/all_to_all | solution.py:322
  18.8 2.0 %copy-start = (bf16[2,2,32,128,128]{4,3,2,1,0:T(8,128)(2,1)}, bf16[2,2,32,128,128]{4,3,2,1,0:T(8,128)(2,1)S(1)}, u32[]{:S(2)}) copy-start(bf16[2,2,32,128,128]{4,3,2,1,0:T(8,128)(2,1)S(1)} %fetch_early.1.early_ref) | copy-start | bytes 12582916
  20.8 10.2 %collective-permute-start.5 = (bf16[48,1024]{1,0:T(8,128)(2,1)S(1)}, bf16[48,1024]{1,0:T(8,128)(2,1)S(1)}, u32[]{:S(2)}, u32[]{:S(2)}) collective-permute-start(bf16[48,1024]{1,0:T(8,128)(2,1)S(1)} %collective-permute-done.1), channel_id=1, source_target_pairs={{0,16},{16,0},{32,48},{48,32},{64,80},{80,64},{96,112},{112,96},{1... | collective-permute-start | bytes 294920 | tf_op jit(solution)/shard_map/ppermute | solution.py:331
  21.0 10.0 %collective-permute-start.6 = (bf16[48,1024]{1,0:T(8,128)(2,1)S(1)}, bf16[48,1024]{1,0:T(8,128)(2,1)S(1)}, u32[]{:S(2)}, u32[]{:S(2)}) collective-permute-start(bf16[48,1024]{1,0:T(8,128)(2,1)S(1)} %collective-permute-done.2), channel_id=1, source_target_pairs={{0,16},{16,0},{32,48},{48,32},{64,80},{80,64},{96,112},{112,96},{1... | collective-permute-start | bytes 294920 | tf_op jit(solution)/shard_map/ppermute | solution.py:331
  21.3 9.8 %collective-permute-start.7 = (bf16[48,1024]{1,0:T(8,128)(2,1)S(1)}, bf16[48,1024]{1,0:T(8,128)(2,1)S(1)}, u32[]{:S(2)}, u32[]{:S(2)}) collective-permute-start(bf16[48,1024]{1,0:T(8,128)(2,1)S(1)} %collective-permute-done.3), channel_id=1, source_target_pairs={{0,16},{16,0},{32,48},{48,32},{64,80},{80,64},{96,112},{112,96},{1... | collective-permute-start | bytes 294920 | tf_op jit(solution)/shard_map/ppermute | solution.py:331
  31.0 2.3 %collective-permute-start = (bf16[16,24,1024]{2,1,0:T(8,128)(2,1)S(1)}, bf16[16,24,1024]{2,1,0:T(8,128)(2,1)S(1)}, u32[]{:S(2)}, u32[]{:S(2)}) collective-permute-start(bf16[16,24,1024]{2,1,0:T(8,128)(2,1)S(1)} %all-to-all-done.own_ref), channel_id=1, source_target_pairs={{0,16},{16,0},{32,48},{48,32},{64,80},{80,64},{96,112},{112,96},{1... | collective-permute-start | bytes 2359304 | tf_op jit(solution)/shard_map/ppermute | solution.py:334
  33.3 2.2 %copy-start.1 = (bf16[2,2,32,128,128]{4,3,2,1,0:T(8,128)(2,1)S(1)}, bf16[2,2,32,128,128]{4,3,2,1,0:T(8,128)(2,1)}, u32[]{:S(2)}) copy-start(bf16[2,2,32,128,128]{4,3,2,1,0:T(8,128)(2,1)} %copy-done) | copy-start | bytes 12582916
  42.9 14.9 %all-to-all-start.1 = ((f32[16,56,128]{2,1,0:T(8,128)}), f32[16,56,128]{2,1,0:T(8,128)S(1)}, u32[]{:S(2)}, u32[]{:S(2)}) async-start(f32[16,56,128]{2,1,0:T(8,128)} %tile_rows.1), calls=%async_computation.1 | async-start | bytes 917504 | tf_op jit(solution)/shard_map/all_to_all | solution.py:338

commit v3 on v2

--- a/solution.py
+++ b/solution.py
@@ -202,8 +202,13 @@
                 block = mode1_ref[2 * pair + side]
                 slot = lax.rem(lax.div(block, IB_DEV), owners)
                 offset = lax.rem(block, IB_DEV).astype(F32)
-                send_ref[slot, 0:rank, :] = flipped[side * rank : (side + 1) * rank, :]
-                send_ref[slot, rank : rank + META, :] = jnp.full((META, edge), offset, F32)
+                rows = flipped[side * rank : (side + 1) * rank, :]
+                high = rows.astype(BF16)
+                send_ref[slot, 0:rank, :] = high
+                send_ref[slot, rank : 2 * rank, :] = (rows - high.astype(F32)).astype(BF16)
+                send_ref[slot, 2 * rank : 2 * rank + META, :] = jnp.full(
+                    (META, edge), offset, F32
+                ).astype(BF16)
 
 
 def tile_rows(mode1, mode2, mode3, row, own, other, three, early, tiles):
@@ -214,7 +219,7 @@
         rows_kernel,
         in_specs=[SMEM] * 4 + [VMEM] * 4 + [HBM],
         out_specs=VMEM,
-        out_shape=jax.ShapeDtypeStruct((owners, 2 * half + META, edge), F32),
+        out_shape=jax.ShapeDtypeStruct((owners, 4 * half + META, edge), BF16),
         scratch_shapes=[
             pltpu.VMEM((tile_count // 2, 128, 2 * edge), BF16),
             pltpu.VMEM((late, 2, edge // CHUNKS, edge, edge), BF16),
@@ -282,13 +287,16 @@
 def solve_kernel(received_ref, inverse_ref, out_ref, side_ref):
     owners, _, edge = received_ref.shape
     rank = inverse_ref.shape[0]
+    totals = [jnp.zeros((rank // 8, 8, edge), F32) for _ in range(IB_DEV)]
+    for owner in range(owners):
+        offsets = received_ref[owner, 2 * rank : 2 * rank + META, :].astype(F32)[None]
+        high = received_ref[owner, 0:rank, :].astype(F32)
+        low = received_ref[owner, rank : 2 * rank, :].astype(F32)
+        rows = (high + low).reshape(rank // 8, 8, edge)
+        for offset in range(IB_DEV):
+            totals[offset] += jnp.where(offsets == float(offset), rows, 0.0)
     for offset in range(IB_DEV):
-        total = jnp.zeros((rank // 8, 8, edge), F32)
-        for owner in range(owners):
-            hit = (received_ref[owner, rank : rank + META, :] == float(offset))[None]
-            rows = received_ref[owner, 0:rank, :].reshape(rank // 8, 8, edge)
-            total += jnp.where(hit, rows, 0.0)
-        side_ref[:, offset * edge : (offset + 1) * edge] = total.reshape(rank, edge)
+        side_ref[:, offset * edge : (offset + 1) * edge] = totals[offset].reshape(rank, edge)
     out_ref[...] = jnp.dot(
         inverse_ref[...],
         side_ref[...],

time: 59.4 us -> 59.2 us (level)
  no operation moved by 1% of the time
where the time goes in v3:
time: 59.2 us; the launch traced here: 58.7 us
  starting transfers between devices  18.2 us (31%)
  waiting for transfers between devices  17.6 us (30%)
  Pallas kernels  15.9 us (27%)
  local copies, waits for them, and re-layouts  6.1 us (10%)
  other arithmetic  0.83 us (1%)
    all_to_all x1, waiting for transfers between devices, update(): lax.all_to_all(jnp.broadcast_to(mine[None], (cols, half, width)), 'col',...  9.42 us
    all_to_all x1, starting transfers between devices, update(): lax.all_to_all(jnp.broadcast_to(mine[None], (cols, half, width)), 'col',...  7.88 us
    pallas_call x1, Pallas kernels, tile_rows(): pl.pallas_call(rows_kernel, in_specs=[SMEM] * 4 + [VMEM] * 4 + [HBM], out...  7.42 us
    ppermute x3, starting transfers between devices, update(): near.append(lax.ppermute(factor_mode3, 'row', shift))  6.01 us
    all_to_all x1, waiting for transfers between devices, update(): received = lax.all_to_all(send, 'col', 0, 0, tiled=True)  5.96 us
    unnamed x17, local copies, waits for them, and re-layouts  5.1 us
    pallas_call x1, Pallas kernels, system_inverse(): pl.pallas_call(inverse_kernel, in_specs=[SMEM, VMEM, VMEM, VMEM], out_spe...  5.01 us
    all_to_all x1, starting transfers between devices, update(): received = lax.all_to_all(send, 'col', 0, 0, tiled=True)  3.59 us
  transfers between devices with their start and end apart: 10, of which 3 were waited for; matrix products, arithmetic and copies ran while one was open for 5% of the time, Pallas kernels for 12%

profile of v3, /device:TPU:0, one launch (start us, length us, event | category | flops | bytes accessed | tf_op | source)
XLA Modules:
  0.0 58.7 jit_solution(8654489243652156387)
XLA Ops:
  0.0 1.8 %collective-permute-start.1 = (bf16[48,1024]{1,0:T(8,128)(2,1)}, bf16[48,1024]{1,0:T(8,128)(2,1)S(1)}, u32[]{:S(2)}, u32[]{:S(2)}) collective-permute-start(bf16[48,1024]{1,0:T(8,128)(2,1)} %param.11), channel_id=1, source_target_pairs={{0,32},{16,48},{32,64},{48,80},{64,96},{80,112},{96,0},{112,16},{1... | collective-permute-start | bytes 294920 | tf_op jit(solution)/shard_map/ppermute | solution.py:336
  1.8 2.9 %collective-permute-start.2 = (bf16[48,1024]{1,0:T(8,128)(2,1)}, bf16[48,1024]{1,0:T(8,128)(2,1)S(1)}, u32[]{:S(2)}, u32[]{:S(2)}) collective-permute-start(bf16[48,1024]{1,0:T(8,128)(2,1)} %param.11), channel_id=1, source_target_pairs={{0,64},{16,80},{32,96},{48,112},{64,0},{80,16},{96,32},{112,48},{1... | collective-permute-start | bytes 294920 | tf_op jit(solution)/shard_map/ppermute | solution.py:336
  4.7 1.3 %collective-permute-start.3 = (bf16[48,1024]{1,0:T(8,128)(2,1)}, bf16[48,1024]{1,0:T(8,128)(2,1)S(1)}, u32[]{:S(2)}, u32[]{:S(2)}) collective-permute-start(bf16[48,1024]{1,0:T(8,128)(2,1)} %param.11), channel_id=1, source_target_pairs={{0,96},{16,112},{32,0},{48,16},{64,32},{80,48},{96,64},{112,80},{1... | collective-permute-start | bytes 294920 | tf_op jit(solution)/shard_map/ppermute | solution.py:336
  6.0 0.0 collective-permute-start.4
  6.0 0.8 %slice_select_fusion = bf16[24,1024]{1,0:T(8,128)(2,1)S(1)} fusion(bf16[48,1024]{1,0:T(8,128)(2,1)} %param.10, pred[]{:T(512)S(6)} %eq.3), kind=kLoop, calls=%fused_computation.8 | loop fusion | flops 24576 | bytes 147457 | tf_op jit(solution)/shard_map/jit(_where)/select_n | solution.py:328
  6.9 1.0 %broadcast_in_dim.10 = bf16[16,24,1024]{2,1,0:T(8,128)(2,1)} broadcast(bf16[24,1024]{1,0:T(8,128)(2,1)S(1)} %slice_select_fusion), dimensions={1,2} | broadcast | bytes 835584 | tf_op jit(solution)/shard_map/broadcast_in_dim | solution.py:330
  7.8 7.9 %all-to-all-start = ((bf16[16,24,1024]{2,1,0:T(8,128)(2,1)}), bf16[16,24,1024]{2,1,0:T(8,128)(2,1)S(1)}, u32[]{:S(2)}, u32[]{:S(2)}) async-start(bf16[16,24,1024]{2,1,0:T(8,128)(2,1)} %broadcast_in_dim.10), calls=%async_computation | async-start | bytes 1572864 | tf_op jit(solution)/shard_map/all_to_all | solution.py:330
  15.7 0.9 %bitcast_dynamic-update-slice_fusion.7 = bf16[8,48,1024]{2,1,0:T(8,128)(2,1)S(1)} fusion(bf16[48,1024]{1,0:T(8,128)(2,1)} %param.11), kind=kLoop, calls=%fused_computation.7 | loop fusion | bytes 196608
  16.6 2.2 %fetch_early.1.early_ref = bf16[2,2,32,128,128]{4,3,2,1,0:T(8,128)(2,1)S(1)} custom-call(bf16[4,128,128,128]{3,2,1,0:T(8,128)(2,1)} %tiles_ref.3), custom_call_target="tpu_custom_call" | custom-call | bytes 8388608 | tf_op jit(solution)/shard_map/fetch_early/pallas_call | solution.py:47
  18.8 0.0 copy-start
  18.8 2.0 %copy-done = bf16[2,2,32,128,128]{4,3,2,1,0:T(8,128)(2,1)} copy-done((bf16[2,2,32,128,128]{4,3,2,1,0:T(8,128)(2,1)}, bf16[2,2,32,128,128]{4,3,2,1,0:T(8,128)(2,1)S(1)}, u32[]{:S(2)}) %copy-start) | copy-done | bytes 4194328
  20.8 0.0 collective-permute-done.1
  20.8 0.2 collective-permute-start.5
  21.0 0.0 collective-permute-done.2
  21.0 0.3 collective-permute-start.6
  21.3 0.0 collective-permute-done.3
  21.3 0.2 collective-permute-start.7
  21.6 9.4 %all-to-all-done.own_ref = bf16[16,24,1024]{2,1,0:T(8,128)(2,1)S(1)} async-done(((bf16[16,24,1024]{2,1,0:T(8,128)(2,1)}), bf16[16,24,1024]{2,1,0:T(8,128)(2,1)S(1)}, u32[]{:S(2)}, u32[]{:S(2)}) %all-to-all-start) | async-done | bytes 786464 | tf_op jit(solution)/shard_map/all_to_all | solution.py:330
  31.0 0.0 collective-permute-start
  31.0 0.0 collective-permute-done.4
  31.0 0.0 collective-permute-done.5
  31.1 0.0 collective-permute-done.6
  31.1 0.0 collective-permute-done.7
  31.1 2.2 %collective-permute-done.other_ref = bf16[16,24,1024]{2,1,0:T(8,128)(2,1)S(1)} collective-permute-done((bf16[16,24,1024]{2,1,0:T(8,128)(2,1)S(1)}, bf16[16,24,1024]{2,1,0:T(8,128)(2,1)S(1)}, u32[]{:S(2)}, u32[]{:S(2)}) %collective-permute-start) | collective-permute-done | bytes 786464 | tf_op jit(solution)/shard_map/ppermute | solution.py:342
  33.3 0.0 copy-done.2
  33.3 0.0 copy-done.3
  33.3 2.2 %copy-done.1 = bf16[2,2,32,128,128]{4,3,2,1,0:T(8,128)(2,1)S(1)} copy-done((bf16[2,2,32,128,128]{4,3,2,1,0:T(8,128)(2,1)S(1)}, bf16[2,2,32,128,128]{4,3,2,1,0:T(8,128)(2,1)}, u32[]{:S(2)}) %copy-start.1) | copy-done | bytes 4194328
  35.5 7.4 %tile_rows.1 = bf16[16,104,128]{2,1,0:T(8,128)(2,1)} custom-call(s32[4]{0:T(128)S(1)} %copy-done.2, s32[4]{0:T(128)S(1)} %copy-done.3, s32[4]{0:T(128)S(1)} %copy-done.4, s32[1]{0:T(128)} %bitcast.row_id_ref, bf16[16,24,1024]{2,1,0:T(8,128)(2,1)S(1)} %all-to-all-done.own_ref, bf16[16,24,1024]{2,1,0:T(8,128)(2,1)S(1)} %collective-permute-done.other_ref, ...), custom_call_target="tpu_custom_call" | custom-call | flops 4294967296 | bytes 16777216 | tf_op jit(solution)/shard_map/tile_rows/pallas_call | solution.py:218
  42.9 3.6 %all-to-all-start.1 = ((bf16[16,104,128]{2,1,0:T(8,128)(2,1)}), bf16[16,104,128]{2,1,0:T(8,128)(2,1)S(1)}, u32[]{:S(2)}, u32[]{:S(2)}) async-start(bf16[16,104,128]{2,1,0:T(8,128)(2,1)} %tile_rows.1), calls=%async_computation.1 | async-start | bytes 851968 | tf_op jit(solution)/shard_map/all_to_all | solution.py:346
  46.5 5.0 %system_inverse.1.inverse_ref = f32[48,48]{1,0:T(8,128)S(1)} custom-call(s32[1]{0:T(128)} %bitcast.row_id_ref, bf16[16,24,1024]{2,1,0:T(8,128)(2,1)S(1)} %all-to-all-done.own_ref, bf16[16,24,1024]{2,1,0:T(8,128)(2,1)S(1)} %collective-permute-done.other_ref, bf16[8,48,1024]{2,1,0:T(8,128)(2,1)S(1)} %bitcast_dynamic-update-slice_fusion.three_ref), custom_call_target="tpu_custom_call" | custom-call | flops 8388608 | bytes 16777216 | tf_op jit(solution)/shard_map/system_inverse/pallas_call | solution.py:276
  51.5 6.0 %all-to-all-done.1.received_ref = bf16[16,104,128]{2,1,0:T(8,128)(2,1)S(1)} async-done(((bf16[16,104,128]{2,1,0:T(8,128)(2,1)}), bf16[16,104,128]{2,1,0:T(8,128)(2,1)S(1)}, u32[]{:S(2)}, u32[]{:S(2)}) %all-to-all-start.1) | async-done | bytes 426016 | tf_op jit(solution)/shard_map/all_to_all | solution.py:346
  57.5 1.2 %solve.1 = f32[48,1024]{1,0:T(8,128)} custom-call(bf16[16,104,128]{2,1,0:T(8,128)(2,1)S(1)} %all-to-all-done.1.received_ref, f32[48,48]{1,0:T(8,128)S(1)} %system_inverse.1.inverse_ref), custom_call_target="tpu_custom_call" | custom-call | tf_op jit(solution)/shard_map/solve/pallas_call | solution.py:311
  (12 shorter events, 0.1 us)
Async XLA Ops:
  0.0 33.3 %copy-start.2 = (s32[4]{0:T(128)S(1)}, s32[4]{0:T(128)}, u32[]{:S(2)}) copy-start(s32[4]{0:T(128)} %mode1_ref.1) | copy-start | bytes 52
  0.0 33.3 %copy-start.3 = (s32[4]{0:T(128)S(1)}, s32[4]{0:T(128)}, u32[]{:S(2)}) copy-start(s32[4]{0:T(128)} %mode2_ref.1) | copy-start | bytes 52
  0.0 33.3 %copy-start.4 = (s32[4]{0:T(128)S(1)}, s32[4]{0:T(128)}, u32[]{:S(2)}) copy-start(s32[4]{0:T(128)} %mode3_ref.1) | copy-start | bytes 52
  0.0 20.8 %collective-permute-start.1 = (bf16[48,1024]{1,0:T(8,128)(2,1)}, bf16[48,1024]{1,0:T(8,128)(2,1)S(1)}, u32[]{:S(2)}, u32[]{:S(2)}) collective-permute-start(bf16[48,1024]{1,0:T(8,128)(2,1)} %param.11), channel_id=1, source_target_pairs={{0,32},{16,48},{32,64},{48,80},{64,96},{80,112},{96,0},{112,16},{1... | collective-permute-start | bytes 294920 | tf_op jit(solution)/shard_map/ppermute | solution.py:336
  1.8 19.3 %collective-permute-start.2 = (bf16[48,1024]{1,0:T(8,128)(2,1)}, bf16[48,1024]{1,0:T(8,128)(2,1)S(1)}, u32[]{:S(2)}, u32[]{:S(2)}) collective-permute-start(bf16[48,1024]{1,0:T(8,128)(2,1)} %param.11), channel_id=1, source_target_pairs={{0,64},{16,80},{32,96},{48,112},{64,0},{80,16},{96,32},{112,48},{1... | collective-permute-start | bytes 294920 | tf_op jit(solution)/shard_map/ppermute | solution.py:336
  4.7 16.7 %collective-permute-start.3 = (bf16[48,1024]{1,0:T(8,128)(2,1)}, bf16[48,1024]{1,0:T(8,128)(2,1)S(1)}, u32[]{:S(2)}, u32[]{:S(2)}) collective-permute-start(bf16[48,1024]{1,0:T(8,128)(2,1)} %param.11), channel_id=1, source_target_pairs={{0,96},{16,112},{32,0},{48,16},{64,32},{80,48},{96,64},{112,80},{1... | collective-permute-start | bytes 294920 | tf_op jit(solution)/shard_map/ppermute | solution.py:336
  6.0 25.0 %collective-permute-start.4 = (bf16[48,1024]{1,0:T(8,128)(2,1)}, bf16[48,1024]{1,0:T(8,128)(2,1)S(1)}, u32[]{:S(2)}, u32[]{:S(2)}) collective-permute-start(bf16[48,1024]{1,0:T(8,128)(2,1)} %param.11), channel_id=1, source_target_pairs={{0,16},{16,0},{32,48},{48,32},{64,80},{80,64},{96,112},{112,96},{1... | collective-permute-start | bytes 294920 | tf_op jit(solution)/shard_map/ppermute | solution.py:339
  7.8 23.2 %all-to-all-start = ((bf16[16,24,1024]{2,1,0:T(8,128)(2,1)}), bf16[16,24,1024]{2,1,0:T(8,128)(2,1)S(1)}, u32[]{:S(2)}, u32[]{:S(2)}) async-start(bf16[16,24,1024]{2,1,0:T(8,128)(2,1)} %broadcast_in_dim.10), calls=%async_computation | async-start | bytes 1572864 | tf_op jit(solution)/shard_map/all_to_all | solution.py:330
  18.8 2.0 %copy-start = (bf16[2,2,32,128,128]{4,3,2,1,0:T(8,128)(2,1)}, bf16[2,2,32,128,128]{4,3,2,1,0:T(8,128)(2,1)S(1)}, u32[]{:S(2)}) copy-start(bf16[2,2,32,128,128]{4,3,2,1,0:T(8,128)(2,1)S(1)} %fetch_early.1.early_ref) | copy-start | bytes 12582916
  20.8 10.2 %collective-permute-start.5 = (bf16[48,1024]{1,0:T(8,128)(2,1)S(1)}, bf16[48,1024]{1,0:T(8,128)(2,1)S(1)}, u32[]{:S(2)}, u32[]{:S(2)}) collective-permute-start(bf16[48,1024]{1,0:T(8,128)(2,1)S(1)} %collective-permute-done.1), channel_id=1, source_target_pairs={{0,16},{16,0},{32,48},{48,32},{64,80},{80,64},{96,112},{112,96},{1... | collective-permute-start | bytes 294920 | tf_op jit(solution)/shard_map/ppermute | solution.py:339
  21.0 10.0 %collective-permute-start.6 = (bf16[48,1024]{1,0:T(8,128)(2,1)S(1)}, bf16[48,1024]{1,0:T(8,128)(2,1)S(1)}, u32[]{:S(2)}, u32[]{:S(2)}) collective-permute-start(bf16[48,1024]{1,0:T(8,128)(2,1)S(1)} %collective-permute-done.2), channel_id=1, source_target_pairs={{0,16},{16,0},{32,48},{48,32},{64,80},{80,64},{96,112},{112,96},{1... | collective-permute-start | bytes 294920 | tf_op jit(solution)/shard_map/ppermute | solution.py:339
  21.3 9.8 %collective-permute-start.7 = (bf16[48,1024]{1,0:T(8,128)(2,1)S(1)}, bf16[48,1024]{1,0:T(8,128)(2,1)S(1)}, u32[]{:S(2)}, u32[]{:S(2)}) collective-permute-start(bf16[48,1024]{1,0:T(8,128)(2,1)S(1)} %collective-permute-done.3), channel_id=1, source_target_pairs={{0,16},{16,0},{32,48},{48,32},{64,80},{80,64},{96,112},{112,96},{1... | collective-permute-start | bytes 294920 | tf_op jit(solution)/shard_map/ppermute | solution.py:339
  31.0 2.3 %collective-permute-start = (bf16[16,24,1024]{2,1,0:T(8,128)(2,1)S(1)}, bf16[16,24,1024]{2,1,0:T(8,128)(2,1)S(1)}, u32[]{:S(2)}, u32[]{:S(2)}) collective-permute-start(bf16[16,24,1024]{2,1,0:T(8,128)(2,1)S(1)} %all-to-all-done.own_ref), channel_id=1, source_target_pairs={{0,16},{16,0},{32,48},{48,32},{64,80},{80,64},{96,112},{112,96},{1... | collective-permute-start | bytes 2359304 | tf_op jit(solution)/shard_map/ppermute | solution.py:342
  33.3 2.2 %copy-start.1 = (bf16[2,2,32,128,128]{4,3,2,1,0:T(8,128)(2,1)S(1)}, bf16[2,2,32,128,128]{4,3,2,1,0:T(8,128)(2,1)}, u32[]{:S(2)}) copy-start(bf16[2,2,32,128,128]{4,3,2,1,0:T(8,128)(2,1)} %copy-done) | copy-start | bytes 12582916
  42.9 14.6 %all-to-all-start.1 = ((bf16[16,104,128]{2,1,0:T(8,128)(2,1)}), bf16[16,104,128]{2,1,0:T(8,128)(2,1)S(1)}, u32[]{:S(2)}, u32[]{:S(2)}) async-start(bf16[16,104,128]{2,1,0:T(8,128)(2,1)} %tile_rows.1), calls=%async_computation.1 | async-start | bytes 851968 | tf_op jit(solution)/shard_map/all_to_all | solution.py:346

commit v4 on v3

--- a/solution.py
+++ b/solution.py
@@ -17,6 +17,19 @@
 HBM = pl.BlockSpec(memory_space=pltpu.HBM)
 SMEM = pl.BlockSpec(memory_space=pltpu.SMEM)
 MIB = 1 << 20
+
+
+SIDE = 4
+
+
+def exchange_order(cols):
+    lines = cols // SIDE
+    return [x * SIDE + z for z in reversed(range(SIDE)) for x in reversed(range(lines))]
+
+
+def exchange_slot(owner, cols):
+    lines = cols // SIDE
+    return (SIDE - 1 - lax.rem(owner, SIDE)) * lines + (lines - 1 - lax.div(owner, SIDE))
 
 
 CHUNKS = 4
@@ -165,6 +178,7 @@
                 three_ref[owner, :, span]
             )
             owner, span = place(mode2_ref[2 * pair + side])
+            owner = exchange_slot(owner, owners)
             own = own_ref[owner, :, span].astype(F32)
             other = other_ref[owner, :, span].astype(F32)
             parts.extend(half_rows(own, other, first))
@@ -200,7 +214,7 @@
             flipped = row_ref[...].T
             for side in range(2):
                 block = mode1_ref[2 * pair + side]
-                slot = lax.rem(lax.div(block, IB_DEV), owners)
+                slot = exchange_slot(lax.rem(lax.div(block, IB_DEV), owners), owners)
                 offset = lax.rem(block, IB_DEV).astype(F32)
                 rows = flipped[side * rank : (side + 1) * rank, :]
                 high = rows.astype(BF16)
@@ -327,7 +341,14 @@
     core = lax.rem(row, 2)
     mine = jnp.where(core == 0, factor_mode2[:half], factor_mode2[half:])
     tiles = pltpu.with_memory_space_constraint(tensor_tiles, pltpu.HBM)
-    own = lax.all_to_all(jnp.broadcast_to(mine[None], (cols, half, width)), "col", 0, 0, tiled=True)
+    own = lax.all_to_all(
+        jnp.broadcast_to(mine[None], (cols, half, width)),
+        "col",
+        0,
+        0,
+        tiled=True,
+        axis_index_groups=[exchange_order(cols)],
+    )
     devices = lax.axis_size("row")
     chips = devices // 2
     near, far = [factor_mode3], []
@@ -343,7 +364,9 @@
     early = fetch_early(tiles)
     row_id = row[None]
     send = tile_rows(tile_mode1, tile_mode2, tile_mode3, row_id, own, other, three, early, tiles)
-    received = lax.all_to_all(send, "col", 0, 0, tiled=True)
+    received = lax.all_to_all(
+        send, "col", 0, 0, tiled=True, axis_index_groups=[exchange_order(cols)]
+    )
     inverse = system_inverse(row_id, own, other, three)
     return solve(received, inverse)
 

time: 59.2 us -> 57.3 us (0.968)
  waiting for transfers between devices: 17.6 us -> 10.1 us
  starting transfers between devices: 18.2 us -> 23.8 us
    all_to_all x1, waiting for transfers between devices: 5.96 us -> 1.91 us  [update(): lax.all_to_all(send, 'col', 0, 0, tiled=True, axis_index_groups=[exchange...]
    all_to_all x1, starting transfers between devices: 3.59 us -> 7.35 us  [update(): lax.all_to_all(send, 'col', 0, 0, tiled=True, axis_index_groups=[exchange...]
    all_to_all x1, waiting for transfers between devices: 9.42 us -> 5.96 us  [update(): lax.all_to_all(jnp.broadcast_to(mine[None], (cols, half, width)), 'col',...]
    all_to_all x1, starting transfers between devices: 7.88 us -> 9.73 us  [update(): lax.all_to_all(jnp.broadcast_to(mine[None], (cols, half, width)), 'col',...]
  transfers between devices with their start and end apart: 10 -> 10, of which waited for: 3 -> 3; matrix products, arithmetic and copies ran while one was open for 5% -> 5% of each run, Pallas kernels for 12% -> 13%
where the time goes in v4:
time: 57.3 us; the launch traced here: 56.8 us
  starting transfers between devices  23.8 us (42%)
  Pallas kernels  15.9 us (28%)
  waiting for transfers between devices  10.1 us (18%)
  local copies, waits for them, and re-layouts  6.09 us (11%)
  other arithmetic  0.83 us (1%)
    all_to_all x1, starting transfers between devices, update(): lax.all_to_all(jnp.broadcast_to(mine[None], (cols, half, width)), 'col',...  9.73 us
    pallas_call x1, Pallas kernels, tile_rows(): pl.pallas_call(rows_kernel, in_specs=[SMEM] * 4 + [VMEM] * 4 + [HBM], out...  7.43 us
    all_to_all x1, starting transfers between devices, update(): lax.all_to_all(send, 'col', 0, 0, tiled=True, axis_index_groups=[exchange...  7.35 us
    ppermute x3, starting transfers between devices, update(): near.append(lax.ppermute(factor_mode3, 'row', shift))  6.01 us
    all_to_all x1, waiting for transfers between devices, update(): lax.all_to_all(jnp.broadcast_to(mine[None], (cols, half, width)), 'col',...  5.96 us
    unnamed x17, local copies, waits for them, and re-layouts  5.1 us
    pallas_call x1, Pallas kernels, system_inverse(): pl.pallas_call(inverse_kernel, in_specs=[SMEM, VMEM, VMEM, VMEM], out_spe...  5 us
    pallas_call x1, Pallas kernels, fetch_early(): pl.pallas_call(early_kernel, in_specs=[HBM], out_specs=VMEM, out_shape=ja...  2.2 us
  transfers between devices with their start and end apart: 10, of which 3 were waited for; matrix products, arithmetic and copies ran while one was open for 5% of the time, Pallas kernels for 13%

profile of v4, /device:TPU:0, one launch (start us, length us, event | category | flops | bytes accessed | tf_op | source)
XLA Modules:
  0.0 56.8 jit_solution(5800399377827027616)
XLA Ops:
  0.0 1.8 %collective-permute-start.1 = (bf16[48,1024]{1,0:T(8,128)(2,1)}, bf16[48,1024]{1,0:T(8,128)(2,1)S(1)}, u32[]{:S(2)}, u32[]{:S(2)}) collective-permute-start(bf16[48,1024]{1,0:T(8,128)(2,1)} %param.11), channel_id=1, source_target_pairs={{0,32},{16,48},{32,64},{48,80},{64,96},{80,112},{96,0},{112,16},{1... | collective-permute-start | bytes 294920 | tf_op jit(solution)/shard_map/ppermute | solution.py:357
  1.8 2.9 %collective-permute-start.2 = (bf16[48,1024]{1,0:T(8,128)(2,1)}, bf16[48,1024]{1,0:T(8,128)(2,1)S(1)}, u32[]{:S(2)}, u32[]{:S(2)}) collective-permute-start(bf16[48,1024]{1,0:T(8,128)(2,1)} %param.11), channel_id=1, source_target_pairs={{0,64},{16,80},{32,96},{48,112},{64,0},{80,16},{96,32},{112,48},{1... | collective-permute-start | bytes 294920 | tf_op jit(solution)/shard_map/ppermute | solution.py:357
  4.7 1.3 %collective-permute-start.3 = (bf16[48,1024]{1,0:T(8,128)(2,1)}, bf16[48,1024]{1,0:T(8,128)(2,1)S(1)}, u32[]{:S(2)}, u32[]{:S(2)}) collective-permute-start(bf16[48,1024]{1,0:T(8,128)(2,1)} %param.11), channel_id=1, source_target_pairs={{0,96},{16,112},{32,0},{48,16},{64,32},{80,48},{96,64},{112,80},{1... | collective-permute-start | bytes 294920 | tf_op jit(solution)/shard_map/ppermute | solution.py:357
  6.0 0.0 collective-permute-start.4
  6.0 0.8 %slice_select_fusion = bf16[24,1024]{1,0:T(8,128)(2,1)S(1)} fusion(bf16[48,1024]{1,0:T(8,128)(2,1)} %param.10, pred[]{:T(512)S(6)} %eq.3), kind=kLoop, calls=%fused_computation.8 | loop fusion | flops 24576 | bytes 147457 | tf_op jit(solution)/shard_map/jit(_where)/select_n | solution.py:342
  6.9 1.0 %broadcast_in_dim.10 = bf16[16,24,1024]{2,1,0:T(8,128)(2,1)} broadcast(bf16[24,1024]{1,0:T(8,128)(2,1)S(1)} %slice_select_fusion), dimensions={1,2} | broadcast | bytes 835584 | tf_op jit(solution)/shard_map/broadcast_in_dim | solution.py:345
  7.8 9.7 %all-to-all-start = ((bf16[16,24,1024]{2,1,0:T(8,128)(2,1)}), bf16[16,24,1024]{2,1,0:T(8,128)(2,1)S(1)}, u32[]{:S(2)}, u32[]{:S(2)}) async-start(bf16[16,24,1024]{2,1,0:T(8,128)(2,1)} %broadcast_in_dim.10), calls=%async_computation | async-start | bytes 1572864 | tf_op jit(solution)/shard_map/all_to_all | solution.py:344
  17.6 0.9 %bitcast_dynamic-update-slice_fusion.7 = bf16[8,48,1024]{2,1,0:T(8,128)(2,1)S(1)} fusion(bf16[48,1024]{1,0:T(8,128)(2,1)} %param.11), kind=kLoop, calls=%fused_computation.7 | loop fusion | bytes 196608
  18.5 2.2 %fetch_early.1.early_ref = bf16[2,2,32,128,128]{4,3,2,1,0:T(8,128)(2,1)S(1)} custom-call(bf16[4,128,128,128]{3,2,1,0:T(8,128)(2,1)} %tiles_ref.3), custom_call_target="tpu_custom_call" | custom-call | bytes 8388608 | tf_op jit(solution)/shard_map/fetch_early/pallas_call | solution.py:60
  20.7 0.0 copy-start
  20.7 2.0 %copy-done = bf16[2,2,32,128,128]{4,3,2,1,0:T(8,128)(2,1)} copy-done((bf16[2,2,32,128,128]{4,3,2,1,0:T(8,128)(2,1)}, bf16[2,2,32,128,128]{4,3,2,1,0:T(8,128)(2,1)S(1)}, u32[]{:S(2)}) %copy-start) | copy-done | bytes 4194328
  22.6 0.0 collective-permute-done.1
  22.6 0.2 collective-permute-start.5
  22.9 0.0 collective-permute-done.2
  22.9 0.3 collective-permute-start.6
  23.2 0.0 collective-permute-done.3
  23.2 0.2 collective-permute-start.7
  23.4 6.0 %all-to-all-done.own_ref = bf16[16,24,1024]{2,1,0:T(8,128)(2,1)S(1)} async-done(((bf16[16,24,1024]{2,1,0:T(8,128)(2,1)}), bf16[16,24,1024]{2,1,0:T(8,128)(2,1)S(1)}, u32[]{:S(2)}, u32[]{:S(2)}) %all-to-all-start) | async-done | bytes 786464 | tf_op jit(solution)/shard_map/all_to_all | solution.py:344
  29.4 0.0 collective-permute-start
  29.4 0.0 collective-permute-done.4
  29.4 0.0 collective-permute-done.5
  29.4 0.0 collective-permute-done.6
  29.5 0.0 collective-permute-done.7
  29.5 2.2 %collective-permute-done.other_ref = bf16[16,24,1024]{2,1,0:T(8,128)(2,1)S(1)} collective-permute-done((bf16[16,24,1024]{2,1,0:T(8,128)(2,1)S(1)}, bf16[16,24,1024]{2,1,0:T(8,128)(2,1)S(1)}, u32[]{:S(2)}, u32[]{:S(2)}) %collective-permute-start) | collective-permute-done | bytes 786464 | tf_op jit(solution)/shard_map/ppermute | solution.py:363
  31.7 0.0 copy-done.2
  31.7 0.0 copy-done.3
  31.7 2.2 %copy-done.1 = bf16[2,2,32,128,128]{4,3,2,1,0:T(8,128)(2,1)S(1)} copy-done((bf16[2,2,32,128,128]{4,3,2,1,0:T(8,128)(2,1)S(1)}, bf16[2,2,32,128,128]{4,3,2,1,0:T(8,128)(2,1)}, u32[]{:S(2)}) %copy-start.1) | copy-done | bytes 4194328
  33.9 7.4 %tile_rows.1 = bf16[16,104,128]{2,1,0:T(8,128)(2,1)} custom-call(s32[4]{0:T(128)S(1)} %copy-done.2, s32[4]{0:T(128)S(1)} %copy-done.3, s32[4]{0:T(128)S(1)} %copy-done.4, s32[1]{0:T(128)} %bitcast.row_id_ref, bf16[16,24,1024]{2,1,0:T(8,128)(2,1)S(1)} %all-to-all-done.own_ref, bf16[16,24,1024]{2,1,0:T(8,128)(2,1)S(1)} %collective-permute-done.other_ref, ...), custom_call_target="tpu_custom_call" | custom-call | flops 4294967296 | bytes 16777216 | tf_op jit(solution)/shard_map/tile_rows/pallas_call | solution.py:232
  41.3 7.4 %all-to-all-start.1 = ((bf16[16,104,128]{2,1,0:T(8,128)(2,1)}), bf16[16,104,128]{2,1,0:T(8,128)(2,1)S(1)}, u32[]{:S(2)}, u32[]{:S(2)}) async-start(bf16[16,104,128]{2,1,0:T(8,128)(2,1)} %tile_rows.1), calls=%async_computation.1 | async-start | bytes 851968 | tf_op jit(solution)/shard_map/all_to_all | solution.py:367
  48.7 5.0 %system_inverse.1.inverse_ref = f32[48,48]{1,0:T(8,128)S(1)} custom-call(s32[1]{0:T(128)} %bitcast.row_id_ref, bf16[16,24,1024]{2,1,0:T(8,128)(2,1)S(1)} %all-to-all-done.own_ref, bf16[16,24,1024]{2,1,0:T(8,128)(2,1)S(1)} %collective-permute-done.other_ref, bf16[8,48,1024]{2,1,0:T(8,128)(2,1)S(1)} %bitcast_dynamic-update-slice_fusion.three_ref), custom_call_target="tpu_custom_call" | custom-call | flops 8388608 | bytes 16777216 | tf_op jit(solution)/shard_map/system_inverse/pallas_call | solution.py:290
  53.7 1.9 %all-to-all-done.1.received_ref = bf16[16,104,128]{2,1,0:T(8,128)(2,1)S(1)} async-done(((bf16[16,104,128]{2,1,0:T(8,128)(2,1)}), bf16[16,104,128]{2,1,0:T(8,128)(2,1)S(1)}, u32[]{:S(2)}, u32[]{:S(2)}) %all-to-all-start.1) | async-done | bytes 426016 | tf_op jit(solution)/shard_map/all_to_all | solution.py:367
  55.6 1.2 %solve.1 = f32[48,1024]{1,0:T(8,128)} custom-call(bf16[16,104,128]{2,1,0:T(8,128)(2,1)S(1)} %all-to-all-done.1.received_ref, f32[48,48]{1,0:T(8,128)S(1)} %system_inverse.1.inverse_ref), custom_call_target="tpu_custom_call" | custom-call | tf_op jit(solution)/shard_map/solve/pallas_call | solution.py:325
  (12 shorter events, 0.1 us)
Async XLA Ops:
  0.0 31.7 %copy-start.2 = (s32[4]{0:T(128)S(1)}, s32[4]{0:T(128)}, u32[]{:S(2)}) copy-start(s32[4]{0:T(128)} %mode1_ref.1) | copy-start | bytes 52
  0.0 31.7 %copy-start.3 = (s32[4]{0:T(128)S(1)}, s32[4]{0:T(128)}, u32[]{:S(2)}) copy-start(s32[4]{0:T(128)} %mode2_ref.1) | copy-start | bytes 52
  0.0 31.7 %copy-start.4 = (s32[4]{0:T(128)S(1)}, s32[4]{0:T(128)}, u32[]{:S(2)}) copy-start(s32[4]{0:T(128)} %mode3_ref.1) | copy-start | bytes 52
  0.0 22.6 %collective-permute-start.1 = (bf16[48,1024]{1,0:T(8,128)(2,1)}, bf16[48,1024]{1,0:T(8,128)(2,1)S(1)}, u32[]{:S(2)}, u32[]{:S(2)}) collective-permute-start(bf16[48,1024]{1,0:T(8,128)(2,1)} %param.11), channel_id=1, source_target_pairs={{0,32},{16,48},{32,64},{48,80},{64,96},{80,112},{96,0},{112,16},{1... | collective-permute-start | bytes 294920 | tf_op jit(solution)/shard_map/ppermute | solution.py:357
  1.8 21.1 %collective-permute-start.2 = (bf16[48,1024]{1,0:T(8,128)(2,1)}, bf16[48,1024]{1,0:T(8,128)(2,1)S(1)}, u32[]{:S(2)}, u32[]{:S(2)}) collective-permute-start(bf16[48,1024]{1,0:T(8,128)(2,1)} %param.11), channel_id=1, source_target_pairs={{0,64},{16,80},{32,96},{48,112},{64,0},{80,16},{96,32},{112,48},{1... | collective-permute-start | bytes 294920 | tf_op jit(solution)/shard_map/ppermute | solution.py:357
  4.7 18.5 %collective-permute-start.3 = (bf16[48,1024]{1,0:T(8,128)(2,1)}, bf16[48,1024]{1,0:T(8,128)(2,1)S(1)}, u32[]{:S(2)}, u32[]{:S(2)}) collective-permute-start(bf16[48,1024]{1,0:T(8,128)(2,1)} %param.11), channel_id=1, source_target_pairs={{0,96},{16,112},{32,0},{48,16},{64,32},{80,48},{96,64},{112,80},{1... | collective-permute-start | bytes 294920 | tf_op jit(solution)/shard_map/ppermute | solution.py:357
  6.0 23.4 %collective-permute-start.4 = (bf16[48,1024]{1,0:T(8,128)(2,1)}, bf16[48,1024]{1,0:T(8,128)(2,1)S(1)}, u32[]{:S(2)}, u32[]{:S(2)}) collective-permute-start(bf16[48,1024]{1,0:T(8,128)(2,1)} %param.11), channel_id=1, source_target_pairs={{0,16},{16,0},{32,48},{48,32},{64,80},{80,64},{96,112},{112,96},{1... | collective-permute-start | bytes 294920 | tf_op jit(solution)/shard_map/ppermute | solution.py:360
  7.8 21.6 %all-to-all-start = ((bf16[16,24,1024]{2,1,0:T(8,128)(2,1)}), bf16[16,24,1024]{2,1,0:T(8,128)(2,1)S(1)}, u32[]{:S(2)}, u32[]{:S(2)}) async-start(bf16[16,24,1024]{2,1,0:T(8,128)(2,1)} %broadcast_in_dim.10), calls=%async_computation | async-start | bytes 1572864 | tf_op jit(solution)/shard_map/all_to_all | solution.py:344
  20.7 2.0 %copy-start = (bf16[2,2,32,128,128]{4,3,2,1,0:T(8,128)(2,1)}, bf16[2,2,32,128,128]{4,3,2,1,0:T(8,128)(2,1)S(1)}, u32[]{:S(2)}) copy-start(bf16[2,2,32,128,128]{4,3,2,1,0:T(8,128)(2,1)S(1)} %fetch_early.1.early_ref) | copy-start | bytes 12582916
  22.6 6.8 %collective-permute-start.5 = (bf16[48,1024]{1,0:T(8,128)(2,1)S(1)}, bf16[48,1024]{1,0:T(8,128)(2,1)S(1)}, u32[]{:S(2)}, u32[]{:S(2)}) collective-permute-start(bf16[48,1024]{1,0:T(8,128)(2,1)S(1)} %collective-permute-done.1), channel_id=1, source_target_pairs={{0,16},{16,0},{32,48},{48,32},{64,80},{80,64},{96,112},{112,96},{1... | collective-permute-start | bytes 294920 | tf_op jit(solution)/shard_map/ppermute | solution.py:360
  22.9 6.6 %collective-permute-start.6 = (bf16[48,1024]{1,0:T(8,128)(2,1)S(1)}, bf16[48,1024]{1,0:T(8,128)(2,1)S(1)}, u32[]{:S(2)}, u32[]{:S(2)}) collective-permute-start(bf16[48,1024]{1,0:T(8,128)(2,1)S(1)} %collective-permute-done.2), channel_id=1, source_target_pairs={{0,16},{16,0},{32,48},{48,32},{64,80},{80,64},{96,112},{112,96},{1... | collective-permute-start | bytes 294920 | tf_op jit(solution)/shard_map/ppermute | solution.py:360
  23.2 6.3 %collective-permute-start.7 = (bf16[48,1024]{1,0:T(8,128)(2,1)S(1)}, bf16[48,1024]{1,0:T(8,128)(2,1)S(1)}, u32[]{:S(2)}, u32[]{:S(2)}) collective-permute-start(bf16[48,1024]{1,0:T(8,128)(2,1)S(1)} %collective-permute-done.3), channel_id=1, source_target_pairs={{0,16},{16,0},{32,48},{48,32},{64,80},{80,64},{96,112},{112,96},{1... | collective-permute-start | bytes 294920 | tf_op jit(solution)/shard_map/ppermute | solution.py:360
  29.4 2.3 %collective-permute-start = (bf16[16,24,1024]{2,1,0:T(8,128)(2,1)S(1)}, bf16[16,24,1024]{2,1,0:T(8,128)(2,1)S(1)}, u32[]{:S(2)}, u32[]{:S(2)}) collective-permute-start(bf16[16,24,1024]{2,1,0:T(8,128)(2,1)S(1)} %all-to-all-done.own_ref), channel_id=1, source_target_pairs={{0,16},{16,0},{32,48},{48,32},{64,80},{80,64},{96,112},{112,96},{1... | collective-permute-start | bytes 2359304 | tf_op jit(solution)/shard_map/ppermute | solution.py:363
  31.7 2.2 %copy-start.1 = (bf16[2,2,32,128,128]{4,3,2,1,0:T(8,128)(2,1)S(1)}, bf16[2,2,32,128,128]{4,3,2,1,0:T(8,128)(2,1)}, u32[]{:S(2)}) copy-start(bf16[2,2,32,128,128]{4,3,2,1,0:T(8,128)(2,1)} %copy-done) | copy-start | bytes 12582916
  41.3 14.3 %all-to-all-start.1 = ((bf16[16,104,128]{2,1,0:T(8,128)(2,1)}), bf16[16,104,128]{2,1,0:T(8,128)(2,1)S(1)}, u32[]{:S(2)}, u32[]{:S(2)}) async-start(bf16[16,104,128]{2,1,0:T(8,128)(2,1)} %tile_rows.1), calls=%async_computation.1 | async-start | bytes 851968 | tf_op jit(solution)/shard_map/all_to_all | solution.py:367

commit v5 on v4

--- a/solution.py
+++ b/solution.py
@@ -298,6 +298,15 @@
     )(row, own, other, three)
 
 
+def parts_of(value):
+    parts = []
+    for _ in range(3):
+        part = value.astype(BF16)
+        parts.append(part)
+        value = value - part.astype(F32)
+    return parts
+
+
 def solve_kernel(received_ref, inverse_ref, out_ref, side_ref):
     owners, _, edge = received_ref.shape
     rank = inverse_ref.shape[0]
@@ -311,10 +320,11 @@
             totals[offset] += jnp.where(offsets == float(offset), rows, 0.0)
     for offset in range(IB_DEV):
         side_ref[:, offset * edge : (offset + 1) * edge] = totals[offset].reshape(rank, edge)
+    left, right = parts_of(inverse_ref[...]), parts_of(side_ref[...])
+    pairs = [(0, 0), (0, 1), (1, 0), (1, 1), (0, 2), (2, 0)]
     out_ref[...] = jnp.dot(
-        inverse_ref[...],
-        side_ref[...],
-        precision=lax.Precision.HIGHEST,
+        jnp.concatenate([left[a] for a, _ in pairs], axis=1),
+        jnp.concatenate([right[b] for _, b in pairs], axis=0),
         preferred_element_type=F32,
     )
 

time: 57.3 us -> 57.3 us (level)
  no operation moved by 1% of the time
where the time goes in v5:
time: 57.3 us; the launch traced here: 56.8 us
  starting transfers between devices  23.8 us (42%)
  Pallas kernels  15.8 us (28%)
  waiting for transfers between devices  10.1 us (18%)
  local copies, waits for them, and re-layouts  6.09 us (11%)
  other arithmetic  0.83 us (1%)
    all_to_all x1, starting transfers between devices, update(): lax.all_to_all(jnp.broadcast_to(mine[None], (cols, half, width)), 'col',...  9.73 us
    pallas_call x1, Pallas kernels, tile_rows(): pl.pallas_call(rows_kernel, in_specs=[SMEM] * 4 + [VMEM] * 4 + [HBM], out...  7.43 us
    all_to_all x1, starting transfers between devices, update(): lax.all_to_all(send, 'col', 0, 0, tiled=True, axis_index_groups=[exchange...  7.35 us
    ppermute x3, starting transfers between devices, update(): near.append(lax.ppermute(factor_mode3, 'row', shift))  6.01 us
    all_to_all x1, waiting for transfers between devices, update(): lax.all_to_all(jnp.broadcast_to(mine[None], (cols, half, width)), 'col',...  5.96 us
    unnamed x17, local copies, waits for them, and re-layouts  5.1 us
    pallas_call x1, Pallas kernels, system_inverse(): pl.pallas_call(inverse_kernel, in_specs=[SMEM, VMEM, VMEM, VMEM], out_spe...  5 us
    pallas_call x1, Pallas kernels, fetch_early(): pl.pallas_call(early_kernel, in_specs=[HBM], out_specs=VMEM, out_shape=ja...  2.2 us
  transfers between devices with their start and end apart: 10, of which 3 were waited for; matrix products, arithmetic and copies ran while one was open for 5% of the time, Pallas kernels for 13%

profile of v5, /device:TPU:0, one launch (start us, length us, event | category | flops | bytes accessed | tf_op | source)
XLA Modules:
  0.0 56.8 jit_solution(918123449292177799)
XLA Ops:
  0.0 1.8 %collective-permute-start.1 = (bf16[48,1024]{1,0:T(8,128)(2,1)}, bf16[48,1024]{1,0:T(8,128)(2,1)S(1)}, u32[]{:S(2)}, u32[]{:S(2)}) collective-permute-start(bf16[48,1024]{1,0:T(8,128)(2,1)} %param.11), channel_id=1, source_target_pairs={{0,32},{16,48},{32,64},{48,80},{64,96},{80,112},{96,0},{112,16},{1... | collective-permute-start | bytes 294920 | tf_op jit(solution)/shard_map/ppermute | solution.py:367
  1.8 2.9 %collective-permute-start.2 = (bf16[48,1024]{1,0:T(8,128)(2,1)}, bf16[48,1024]{1,0:T(8,128)(2,1)S(1)}, u32[]{:S(2)}, u32[]{:S(2)}) collective-permute-start(bf16[48,1024]{1,0:T(8,128)(2,1)} %param.11), channel_id=1, source_target_pairs={{0,64},{16,80},{32,96},{48,112},{64,0},{80,16},{96,32},{112,48},{1... | collective-permute-start | bytes 294920 | tf_op jit(solution)/shard_map/ppermute | solution.py:367
  4.7 1.3 %collective-permute-start.3 = (bf16[48,1024]{1,0:T(8,128)(2,1)}, bf16[48,1024]{1,0:T(8,128)(2,1)S(1)}, u32[]{:S(2)}, u32[]{:S(2)}) collective-permute-start(bf16[48,1024]{1,0:T(8,128)(2,1)} %param.11), channel_id=1, source_target_pairs={{0,96},{16,112},{32,0},{48,16},{64,32},{80,48},{96,64},{112,80},{1... | collective-permute-start | bytes 294920 | tf_op jit(solution)/shard_map/ppermute | solution.py:367
  6.0 0.0 collective-permute-start.4
  6.0 0.8 %slice_select_fusion = bf16[24,1024]{1,0:T(8,128)(2,1)S(1)} fusion(bf16[48,1024]{1,0:T(8,128)(2,1)} %param.10, pred[]{:T(512)S(6)} %eq.3), kind=kLoop, calls=%fused_computation.8 | loop fusion | flops 24576 | bytes 147457 | tf_op jit(solution)/shard_map/jit(_where)/select_n | solution.py:352
  6.9 1.0 %broadcast_in_dim.10 = bf16[16,24,1024]{2,1,0:T(8,128)(2,1)} broadcast(bf16[24,1024]{1,0:T(8,128)(2,1)S(1)} %slice_select_fusion), dimensions={1,2} | broadcast | bytes 835584 | tf_op jit(solution)/shard_map/broadcast_in_dim | solution.py:355
  7.8 9.7 %all-to-all-start = ((bf16[16,24,1024]{2,1,0:T(8,128)(2,1)}), bf16[16,24,1024]{2,1,0:T(8,128)(2,1)S(1)}, u32[]{:S(2)}, u32[]{:S(2)}) async-start(bf16[16,24,1024]{2,1,0:T(8,128)(2,1)} %broadcast_in_dim.10), calls=%async_computation | async-start | bytes 1572864 | tf_op jit(solution)/shard_map/all_to_all | solution.py:354
  17.6 0.9 %bitcast_dynamic-update-slice_fusion.7 = bf16[8,48,1024]{2,1,0:T(8,128)(2,1)S(1)} fusion(bf16[48,1024]{1,0:T(8,128)(2,1)} %param.11), kind=kLoop, calls=%fused_computation.7 | loop fusion | bytes 196608
  18.5 2.2 %fetch_early.1.early_ref = bf16[2,2,32,128,128]{4,3,2,1,0:T(8,128)(2,1)S(1)} custom-call(bf16[4,128,128,128]{3,2,1,0:T(8,128)(2,1)} %tiles_ref.3), custom_call_target="tpu_custom_call" | custom-call | bytes 8388608 | tf_op jit(solution)/shard_map/fetch_early/pallas_call | solution.py:60
  20.7 0.0 copy-start
  20.7 2.0 %copy-done = bf16[2,2,32,128,128]{4,3,2,1,0:T(8,128)(2,1)} copy-done((bf16[2,2,32,128,128]{4,3,2,1,0:T(8,128)(2,1)}, bf16[2,2,32,128,128]{4,3,2,1,0:T(8,128)(2,1)S(1)}, u32[]{:S(2)}) %copy-start) | copy-done | bytes 4194328
  22.6 0.0 collective-permute-done.1
  22.6 0.2 collective-permute-start.5
  22.9 0.0 collective-permute-done.2
  22.9 0.3 collective-permute-start.6
  23.2 0.0 collective-permute-done.3
  23.2 0.2 collective-permute-start.7
  23.4 6.0 %all-to-all-done.own_ref = bf16[16,24,1024]{2,1,0:T(8,128)(2,1)S(1)} async-done(((bf16[16,24,1024]{2,1,0:T(8,128)(2,1)}), bf16[16,24,1024]{2,1,0:T(8,128)(2,1)S(1)}, u32[]{:S(2)}, u32[]{:S(2)}) %all-to-all-start) | async-done | bytes 786464 | tf_op jit(solution)/shard_map/all_to_all | solution.py:354
  29.4 0.0 collective-permute-start
  29.4 0.0 collective-permute-done.4
  29.4 0.0 collective-permute-done.5
  29.4 0.0 collective-permute-done.6
  29.5 0.0 collective-permute-done.7
  29.5 2.2 %collective-permute-done.other_ref = bf16[16,24,1024]{2,1,0:T(8,128)(2,1)S(1)} collective-permute-done((bf16[16,24,1024]{2,1,0:T(8,128)(2,1)S(1)}, bf16[16,24,1024]{2,1,0:T(8,128)(2,1)S(1)}, u32[]{:S(2)}, u32[]{:S(2)}) %collective-permute-start) | collective-permute-done | bytes 786464 | tf_op jit(solution)/shard_map/ppermute | solution.py:373
  31.7 0.0 copy-done.2
  31.7 0.0 copy-done.3
  31.7 2.2 %copy-done.1 = bf16[2,2,32,128,128]{4,3,2,1,0:T(8,128)(2,1)S(1)} copy-done((bf16[2,2,32,128,128]{4,3,2,1,0:T(8,128)(2,1)S(1)}, bf16[2,2,32,128,128]{4,3,2,1,0:T(8,128)(2,1)}, u32[]{:S(2)}) %copy-start.1) | copy-done | bytes 4194328
  33.9 7.4 %tile_rows.1 = bf16[16,104,128]{2,1,0:T(8,128)(2,1)} custom-call(s32[4]{0:T(128)S(1)} %copy-done.2, s32[4]{0:T(128)S(1)} %copy-done.3, s32[4]{0:T(128)S(1)} %copy-done.4, s32[1]{0:T(128)} %bitcast.row_id_ref, bf16[16,24,1024]{2,1,0:T(8,128)(2,1)S(1)} %all-to-all-done.own_ref, bf16[16,24,1024]{2,1,0:T(8,128)(2,1)S(1)} %collective-permute-done.other_ref, ...), custom_call_target="tpu_custom_call" | custom-call | flops 4294967296 | bytes 16777216 | tf_op jit(solution)/shard_map/tile_rows/pallas_call | solution.py:232
  41.3 7.4 %all-to-all-start.1 = ((bf16[16,104,128]{2,1,0:T(8,128)(2,1)}), bf16[16,104,128]{2,1,0:T(8,128)(2,1)S(1)}, u32[]{:S(2)}, u32[]{:S(2)}) async-start(bf16[16,104,128]{2,1,0:T(8,128)(2,1)} %tile_rows.1), calls=%async_computation.1 | async-start | bytes 851968 | tf_op jit(solution)/shard_map/all_to_all | solution.py:377
  48.7 5.0 %system_inverse.1.inverse_ref = f32[48,48]{1,0:T(8,128)S(1)} custom-call(s32[1]{0:T(128)} %bitcast.row_id_ref, bf16[16,24,1024]{2,1,0:T(8,128)(2,1)S(1)} %all-to-all-done.own_ref, bf16[16,24,1024]{2,1,0:T(8,128)(2,1)S(1)} %collective-permute-done.other_ref, bf16[8,48,1024]{2,1,0:T(8,128)(2,1)S(1)} %bitcast_dynamic-update-slice_fusion.three_ref), custom_call_target="tpu_custom_call" | custom-call | flops 8388608 | bytes 16777216 | tf_op jit(solution)/shard_map/system_inverse/pallas_call | solution.py:290
  53.7 1.9 %all-to-all-done.1.received_ref = bf16[16,104,128]{2,1,0:T(8,128)(2,1)S(1)} async-done(((bf16[16,104,128]{2,1,0:T(8,128)(2,1)}), bf16[16,104,128]{2,1,0:T(8,128)(2,1)S(1)}, u32[]{:S(2)}, u32[]{:S(2)}) %all-to-all-start.1) | async-done | bytes 426016 | tf_op jit(solution)/shard_map/all_to_all | solution.py:377
  55.6 1.2 %solve.1 = f32[48,1024]{1,0:T(8,128)} custom-call(bf16[16,104,128]{2,1,0:T(8,128)(2,1)S(1)} %all-to-all-done.1.received_ref, f32[48,48]{1,0:T(8,128)S(1)} %system_inverse.1.inverse_ref), custom_call_target="tpu_custom_call" | custom-call | tf_op jit(solution)/shard_map/solve/pallas_call | solution.py:335
  (12 shorter events, 0.1 us)
Async XLA Ops:
  0.0 31.7 %copy-start.2 = (s32[4]{0:T(128)S(1)}, s32[4]{0:T(128)}, u32[]{:S(2)}) copy-start(s32[4]{0:T(128)} %mode1_ref.1) | copy-start | bytes 52
  0.0 31.7 %copy-start.3 = (s32[4]{0:T(128)S(1)}, s32[4]{0:T(128)}, u32[]{:S(2)}) copy-start(s32[4]{0:T(128)} %mode2_ref.1) | copy-start | bytes 52
  0.0 31.7 %copy-start.4 = (s32[4]{0:T(128)S(1)}, s32[4]{0:T(128)}, u32[]{:S(2)}) copy-start(s32[4]{0:T(128)} %mode3_ref.1) | copy-start | bytes 52
  0.0 22.6 %collective-permute-start.1 = (bf16[48,1024]{1,0:T(8,128)(2,1)}, bf16[48,1024]{1,0:T(8,128)(2,1)S(1)}, u32[]{:S(2)}, u32[]{:S(2)}) collective-permute-start(bf16[48,1024]{1,0:T(8,128)(2,1)} %param.11), channel_id=1, source_target_pairs={{0,32},{16,48},{32,64},{48,80},{64,96},{80,112},{96,0},{112,16},{1... | collective-permute-start | bytes 294920 | tf_op jit(solution)/shard_map/ppermute | solution.py:367
  1.8 21.1 %collective-permute-start.2 = (bf16[48,1024]{1,0:T(8,128)(2,1)}, bf16[48,1024]{1,0:T(8,128)(2,1)S(1)}, u32[]{:S(2)}, u32[]{:S(2)}) collective-permute-start(bf16[48,1024]{1,0:T(8,128)(2,1)} %param.11), channel_id=1, source_target_pairs={{0,64},{16,80},{32,96},{48,112},{64,0},{80,16},{96,32},{112,48},{1... | collective-permute-start | bytes 294920 | tf_op jit(solution)/shard_map/ppermute | solution.py:367
  4.7 18.5 %collective-permute-start.3 = (bf16[48,1024]{1,0:T(8,128)(2,1)}, bf16[48,1024]{1,0:T(8,128)(2,1)S(1)}, u32[]{:S(2)}, u32[]{:S(2)}) collective-permute-start(bf16[48,1024]{1,0:T(8,128)(2,1)} %param.11), channel_id=1, source_target_pairs={{0,96},{16,112},{32,0},{48,16},{64,32},{80,48},{96,64},{112,80},{1... | collective-permute-start | bytes 294920 | tf_op jit(solution)/shard_map/ppermute | solution.py:367
  6.0 23.4 %collective-permute-start.4 = (bf16[48,1024]{1,0:T(8,128)(2,1)}, bf16[48,1024]{1,0:T(8,128)(2,1)S(1)}, u32[]{:S(2)}, u32[]{:S(2)}) collective-permute-start(bf16[48,1024]{1,0:T(8,128)(2,1)} %param.11), channel_id=1, source_target_pairs={{0,16},{16,0},{32,48},{48,32},{64,80},{80,64},{96,112},{112,96},{1... | collective-permute-start | bytes 294920 | tf_op jit(solution)/shard_map/ppermute | solution.py:370
  7.8 21.6 %all-to-all-start = ((bf16[16,24,1024]{2,1,0:T(8,128)(2,1)}), bf16[16,24,1024]{2,1,0:T(8,128)(2,1)S(1)}, u32[]{:S(2)}, u32[]{:S(2)}) async-start(bf16[16,24,1024]{2,1,0:T(8,128)(2,1)} %broadcast_in_dim.10), calls=%async_computation | async-start | bytes 1572864 | tf_op jit(solution)/shard_map/all_to_all | solution.py:354
  20.7 2.0 %copy-start = (bf16[2,2,32,128,128]{4,3,2,1,0:T(8,128)(2,1)}, bf16[2,2,32,128,128]{4,3,2,1,0:T(8,128)(2,1)S(1)}, u32[]{:S(2)}) copy-start(bf16[2,2,32,128,128]{4,3,2,1,0:T(8,128)(2,1)S(1)} %fetch_early.1.early_ref) | copy-start | bytes 12582916
  22.6 6.8 %collective-permute-start.5 = (bf16[48,1024]{1,0:T(8,128)(2,1)S(1)}, bf16[48,1024]{1,0:T(8,128)(2,1)S(1)}, u32[]{:S(2)}, u32[]{:S(2)}) collective-permute-start(bf16[48,1024]{1,0:T(8,128)(2,1)S(1)} %collective-permute-done.1), channel_id=1, source_target_pairs={{0,16},{16,0},{32,48},{48,32},{64,80},{80,64},{96,112},{112,96},{1... | collective-permute-start | bytes 294920 | tf_op jit(solution)/shard_map/ppermute | solution.py:370
  22.9 6.6 %collective-permute-start.6 = (bf16[48,1024]{1,0:T(8,128)(2,1)S(1)}, bf16[48,1024]{1,0:T(8,128)(2,1)S(1)}, u32[]{:S(2)}, u32[]{:S(2)}) collective-permute-start(bf16[48,1024]{1,0:T(8,128)(2,1)S(1)} %collective-permute-done.2), channel_id=1, source_target_pairs={{0,16},{16,0},{32,48},{48,32},{64,80},{80,64},{96,112},{112,96},{1... | collective-permute-start | bytes 294920 | tf_op jit(solution)/shard_map/ppermute | solution.py:370
  23.2 6.3 %collective-permute-start.7 = (bf16[48,1024]{1,0:T(8,128)(2,1)S(1)}, bf16[48,1024]{1,0:T(8,128)(2,1)S(1)}, u32[]{:S(2)}, u32[]{:S(2)}) collective-permute-start(bf16[48,1024]{1,0:T(8,128)(2,1)S(1)} %collective-permute-done.3), channel_id=1, source_target_pairs={{0,16},{16,0},{32,48},{48,32},{64,80},{80,64},{96,112},{112,96},{1... | collective-permute-start | bytes 294920 | tf_op jit(solution)/shard_map/ppermute | solution.py:370
  29.4 2.3 %collective-permute-start = (bf16[16,24,1024]{2,1,0:T(8,128)(2,1)S(1)}, bf16[16,24,1024]{2,1,0:T(8,128)(2,1)S(1)}, u32[]{:S(2)}, u32[]{:S(2)}) collective-permute-start(bf16[16,24,1024]{2,1,0:T(8,128)(2,1)S(1)} %all-to-all-done.own_ref), channel_id=1, source_target_pairs={{0,16},{16,0},{32,48},{48,32},{64,80},{80,64},{96,112},{112,96},{1... | collective-permute-start | bytes 2359304 | tf_op jit(solution)/shard_map/ppermute | solution.py:373
  31.7 2.2 %copy-start.1 = (bf16[2,2,32,128,128]{4,3,2,1,0:T(8,128)(2,1)S(1)}, bf16[2,2,32,128,128]{4,3,2,1,0:T(8,128)(2,1)}, u32[]{:S(2)}) copy-start(bf16[2,2,32,128,128]{4,3,2,1,0:T(8,128)(2,1)} %copy-done) | copy-start | bytes 12582916
  41.3 14.3 %all-to-all-start.1 = ((bf16[16,104,128]{2,1,0:T(8,128)(2,1)}), bf16[16,104,128]{2,1,0:T(8,128)(2,1)S(1)}, u32[]{:S(2)}, u32[]{:S(2)}) async-start(bf16[16,104,128]{2,1,0:T(8,128)(2,1)} %tile_rows.1), calls=%async_computation.1 | async-start | bytes 851968 | tf_op jit(solution)/shard_map/all_to_all | solution.py:377
